TPU v7x, 32 devices: a whole 2x2x4 slice. The times are simulated.
32 devices in a mesh: pre: 2 (over y), dec: 4 (over x, core), rep: 4 (over z).
Axes of the slice: x: 2, y: 2, z: 4, core: 2. Of those that a mesh axis runs over, the one named last changes fastest.
Arguments:
- layer_queries: bfloat16 [2048, 8192], P(('pre', 'rep'), 'dec'), may hold values from -16 to 16
- layer_keys: bfloat16 [2048, 1024], P(('pre', 'rep')), may hold values from -16 to 16
- layer_values: bfloat16 [2048, 1024], P(('pre', 'rep')), may hold values from -6 to 6
- query_bias: float32 [8192], P('dec'), may hold values from -3 to 3
- key_bias: float32 [1024], replicated, may hold values from -3 to 3
- value_bias: float32 [1024], replicated, may hold values from -3 to 3
- positions: int32 [2048], replicated, may hold values from 0 to 2047, each once
- lengths: int32 [32], replicated, may hold values from 1 to 1024, as said below
- replica_of: int32 [32], replicated, may hold values from 0 to 3, as said below
- page_table: int32 [4, 16], replicated, may hold values from 0 to 3, as said below
- prefill_cache: bfloat16 [4, 16, 16, 4, 64, 128], P('rep', 'pre', 'dec'), may hold values from -6 to 6
Outputs:
- context: bfloat16 [2048, 8192], P(('pre', 'rep'), 'dec')
- decode_cache: bfloat16 [4, 4, 8, 16, 4, 64, 128], P('rep', 'dec', None, 'pre')
Inputs may be any that keep to these rules, and one draw needn't show every extreme that they name: `replica_of`: each replica receives exactly 8 requests. `lengths`: the requests of each replica fill exactly 16 blocks of 128 tokens, each request starting a new block; in each replica one request spans exactly 8 full blocks. `page_table`: in each aligned run of 8 blocks of a replica, exactly half of the 4 decode devices appear, each exactly 4 times.
All inputs are finite; a program needn't handle non-finite values.
Results may differ from a plain program's by a relative error of at most 0.0094.
Values may be sent and summed in bfloat16 or wider, within the bound.
No kernel may reach another device: no remote copies, remote signals or barrier semaphores. Data moves between devices by JAX's collectives and lax.ppermute only.
A program may use at most 128 MiB of HBM per device.

v0:
```python
import jax
import jax.numpy as jnp
from jax import lax
from jax.sharding import PartitionSpec as P

HEADS = 64
KVH = 8
HD = 128
BLOCK = 128


rope_base = 1000000.0
masked_score = -1e30


def rotate(values, where_at):
    width = values.shape[-1]
    half_width = width // 2
    freqs = 1.0 / rope_base ** (jnp.arange(half_width, dtype=jnp.float32) * (2.0 / width))
    angles = where_at.astype(jnp.float32)[:, None] * freqs[None, :]
    cosine = jnp.cos(angles)[:, None, :]
    sine = jnp.sin(angles)[:, None, :]
    first = values[..., :half_width]
    second = values[..., half_width:]
    return jnp.concatenate(
        [first * cosine - second * sine, second * cosine + first * sine], axis=-1
    )


def valid_tokens(lengths, replica_of, replica, block_ids):
    member = replica_of == replica
    counts = jnp.where(member, (lengths + (BLOCK - 1)) // BLOCK, 0)
    starts = jnp.cumsum(counts) - counts
    inside = (block_ids[:, None] >= starts[None, :]) & (
        block_ids[:, None] < (starts + counts)[None, :]
    )
    remain = lengths[None, :] - BLOCK * (block_ids[:, None] - starts[None, :])
    return jnp.sum(jnp.where(inside, jnp.clip(remain, 0, BLOCK), 0), axis=1)


def shards(
    layer_queries,
    layer_keys,
    layer_values,
    query_bias,
    key_bias,
    value_bias,
    positions,
    lengths,
    replica_of,
    page_table,
    prefill_cache,
):
    row_count = layer_queries.shape[0]
    head_count = layer_queries.shape[1] // HD
    group_size = HEADS // KVH
    kv_local = max(1, head_count // group_size)
    per_group = head_count // kv_local
    scale = HD ** (-0.5)
    row_start = lax.axis_index(("pre", "rep")) * row_count
    query_pos = lax.dynamic_slice_in_dim(positions, row_start, row_count)
    shifted = layer_queries.astype(jnp.float32).reshape(
        row_count, head_count, HD
    ) + query_bias.reshape(head_count, HD)
    rotated = rotate(shifted, query_pos).astype(jnp.bfloat16)
    query_rows = (
        rotated.reshape(row_count, kv_local, per_group, HD)
        .transpose(1, 2, 0, 3)
        .reshape(kv_local, per_group * row_count, HD)
    )
    query_rowpos = jnp.tile(query_pos, per_group)
    kv_first = lax.axis_index("dec") * head_count // group_size
    bias_keys = lax.dynamic_slice_in_dim(key_bias, kv_first * HD, kv_local * HD).reshape(
        kv_local, HD
    )
    bias_values = lax.dynamic_slice_in_dim(value_bias, kv_first * HD, kv_local * HD).reshape(
        kv_local, HD
    )
    own_keys = lax.dynamic_slice_in_dim(layer_keys, kv_first * HD, kv_local * HD, 1)
    own_values = lax.dynamic_slice_in_dim(layer_values, kv_first * HD, kv_local * HD, 1)
    count = own_keys.shape[0]
    shifted_keys = own_keys.astype(jnp.float32).reshape(count, kv_local, HD) + bias_keys
    keys_rot = rotate(shifted_keys, query_pos).astype(jnp.bfloat16).reshape(count, kv_local * HD)
    values_biased = (
        own_values.astype(jnp.float32).reshape(count, kv_local, HD) + bias_values
    ).astype(jnp.bfloat16)
    local_values = values_biased.reshape(count, kv_local * HD)
    best = jnp.full((kv_local, per_group * row_count), masked_score, jnp.float32)
    piece_keys = lax.all_gather(keys_rot, ("pre", "rep"), axis=0, tiled=True)
    piece_values = lax.all_gather(local_values, ("pre", "rep"), axis=0, tiled=True)
    count = piece_keys.shape[0]
    scores = (
        jnp.einsum(
            "kqd,nkd->kqn",
            query_rows,
            piece_keys.reshape(count, kv_local, HD),
            preferred_element_type=jnp.float32,
        )
        * scale
    )
    allowed = positions[None, None, :] <= query_rowpos[None, :, None]
    scores = jnp.where(allowed, scores, masked_score)
    newest = jnp.maximum(best, jnp.max(scores, axis=2))
    weights = jnp.where(allowed, jnp.exp(scores - newest[:, :, None]), 0.0)
    total = jnp.sum(weights, axis=2)
    added = jnp.einsum(
        "kqn,nkd->kqd",
        weights.astype(jnp.bfloat16),
        piece_values.reshape(count, kv_local, HD),
        preferred_element_type=jnp.float32,
    )
    summed = added
    best, total, summed = (newest, total, summed)
    context = (summed / total[:, :, None]).astype(jnp.bfloat16)
    context = (
        context.reshape(kv_local, per_group, row_count, HD)
        .transpose(2, 0, 1, 3)
        .reshape(row_count, head_count * HD)
    )
    local_cache = prefill_cache[0]
    blk_count = local_cache.shape[0]
    dec_size = lax.axis_size("dec")
    pre_size = lax.axis_size("pre")
    capacity = 2 * blk_count // dec_size
    replica = lax.axis_index("rep")
    run_index = lax.axis_index("pre")
    block_ids = run_index * blk_count + jnp.arange(blk_count, dtype=jnp.int32)
    valid = valid_tokens(lengths, replica_of, replica, block_ids)
    keep = (jnp.arange(BLOCK, dtype=jnp.int32)[None, :] < valid[:, None]).astype(jnp.bfloat16)
    masked = local_cache * keep[:, None, None, None, :]
    page_row = lax.dynamic_index_in_dim(page_table, replica, 0, keepdims=False)
    targets = lax.dynamic_slice_in_dim(page_row, run_index * blk_count, blk_count)
    places = jnp.arange(blk_count, dtype=jnp.int32)
    before_me = (targets[None, :] == targets[:, None]) & (places[None, :] < places[:, None])
    ranks = jnp.sum(before_me, axis=1)
    select = (targets[None, None, :] == jnp.arange(dec_size, dtype=jnp.int32)[:, None, None]) & (
        ranks[None, None, :] == jnp.arange(capacity, dtype=jnp.int32)[None, :, None]
    )
    outgoing = jnp.dot(
        select.reshape(dec_size * capacity, blk_count).astype(jnp.bfloat16),
        masked.reshape(blk_count, -1),
        preferred_element_type=jnp.float32,
    ).astype(jnp.bfloat16)
    outgoing = outgoing.reshape((dec_size, capacity) + local_cache.shape[1:])
    group_halves = 2 * KVH // pre_size
    arrived = lax.all_to_all(
        lax.all_to_all(outgoing, "dec", split_axis=0, concat_axis=2, tiled=True),
        "pre",
        split_axis=2,
        concat_axis=0,
        tiled=True,
    )
    decode_cache = arrived.reshape(
        (1, 1, pre_size * capacity, group_halves) + local_cache.shape[2:]
    )
    return (context, decode_cache)


def solution(mesh):
    placed = (
        P(("pre", "rep"), "dec"),
        P(("pre", "rep"), None),
        P(("pre", "rep"), None),
        P("dec"),
        P(),
        P(),
        P(),
        P(),
        P(),
        P(),
        P("rep", "pre", "dec", None, None, None),
    )
    return jax.shard_map(
        shards,
        mesh=mesh,
        in_specs=placed,
        out_specs=(P(("pre", "rep"), "dec"), P("rep", "dec", None, "pre", None, None, None)),
        check_vma=False,
    )
```

profile of v0, /device:TPU:0, one launch (start us, length us, event | category | flops | bytes accessed | tf_op | source)
XLA Modules:
  0.0 157.9 jit_solution(5007270544340099804)
XLA Ops:
  7.3 1.0 dynamic-slice_convert_fusion
  8.4 0.8 dynamic-slice_bitcast_fusion
  9.3 0.8 fusion.14
  10.0 0.3 multiply_cosine_fusion
  10.4 0.7 pad_maximum_fusion.1
  11.1 0.7 compare_select_fusion
  12.0 0.8 select_reduce_fusion
  13.0 3.0 %broadcast_multiply_fusion = bf16[1,8,4,4,64,128]{5,4,3,2,1,0:T(8,128)(2,1)} fusion(bf16[1,8,4,4,64,128]{5,4,3,2,1,0:T(8,128)(2,1)} %param.21, bf16[8,128]{1,0:T(8,128)(2,1)S(1)} %fusion.10), kind=kLoop, calls=%fused_computation.17 | loop fusion | flops 1048576 | bytes 4196352 | tf_op jit(solution)/shard_map/mul | solution.py:130
  16.0 2.5 %mul.158 = bf16[8,131072]{1,0:T(8,128)(2,1)S(1)} reshape(bf16[1,8,4,4,64,128]{5,4,3,2,1,0:T(8,128)(2,1)} %broadcast_multiply_fusion) | data formatting | bytes 4194304 | tf_op jit(solution)/shard_map/mul | solution.py:130
  18.5 0.8 dynamic-slice_bitcast_fusion.1
  19.5 1.2 fusion.6
  20.7 2.7 %copy.81 = bf16[2,8,1024,128]{3,2,1,0:T(8,128)(2,1)} copy(bf16[2,8,1024,128]{3,1,2,0:T(8,128)(2,1)S(1)} %fusion.6) | data formatting | bytes 8388608
  23.4 5.0 %all-to-all-start = ((bf16[4,4,4,4,64,128]{5,4,3,2,1,0:T(8,128)(2,1)}), bf16[4,4,4,4,64,128]{5,4,3,2,1,0:T(8,128)(2,1)}, u32[]{:S(2)}, u32[]{:S(2)}) async-start(bf16[4,4,4,4,64,128]{5,4,3,2,1,0:T(8,128)(2,1)} %bitcast.51), calls=%async_computation | async-start | bytes 8388608 | tf_op jit(solution)/shard_map/all_to_all | solution.py:147
  28.8 0.8 dynamic_slice.24
  29.6 0.8 add_convert_fusion.1
  30.8 0.4 copy.79
  31.4 0.8 subtract_convert_fusion
  32.1 0.3 copy.60
  32.7 4.1 %broadcast_compare_fusion = pred[2048,2048]{0,1:T(8,128)(4,1)} fusion(s32[2048]{0:T(1024)S(1)} %bitcast.63, s32[2048]{0:T(1024)S(1)} %copy-done.4), kind=kLoop, calls=%fused_computation.8 | loop fusion | flops 4194304 | bytes 4210688 | tf_op jit(solution)/shard_map/le | solution.py:101
  36.9 1.6 pad_maximum_fusion
  38.4 15.1 %all-gather.3.cloned.1.call-done = bf16[2048,256]{0,1:T(8,128)(2,1)} async-done(((bf16[256,256]{0,1:T(8,128)(2,1)}), bf16[2048,256]{0,1:T(8,128)(2,1)}) %all-gather.3.cloned.1.call-update) | async-done | bytes 1048592 | tf_op jit(solution)/shard_map/all_gather | solution.py:89
  53.5 16.9 %fusion = (f32[2,2048]{1,0:T(2,128)S(1)}, f32[2,2048,2048]{1,2,0:T(8,128)}) fusion(pred[2048,2048]{0,1:T(8,128)(4,1)} %broadcast_compare_fusion, bf16[2,2048,128]{2,1,0:T(8,128)(2,1)} %bitcast.58, bf16[2048,2,128]{0,2,1:T(8,128)(2,1)} %bitcast.67), kind=kOutput, calls=%fused_computation.3 | convolution fusion | flops 2172645376 | bytes 39862272 | tf_op jit(solution)/shard_map/kqd,nkd->kqn/dot_general | solution.py:93
  70.4 15.2 %fusion.1 = f32[2,2048]{1,0:T(2,128)S(1)} fusion(f32[2,2048,2048]{1,2,0:T(8,128)} %get-tuple-element.11, f32[2,2048]{1,0:T(2,128)S(1)} %broadcast_maximum_fusion, pred[2048,2048]{0,1:T(8,128)(4,1)S(1)} %copy-done.2), kind=kLoop, calls=%fused_computation.4 | loop fusion | flops 41938944 | bytes 37781504 | tf_op jit(solution)/shard_map/reduce_sum | solution.py:105
  85.7 3.2 %copy.69 = bf16[4,4,4,4,64,128]{5,4,3,2,0,1:T(8,128)(2,1)S(1)} copy(bf16[4,4,4,4,64,128]{5,4,3,2,1,0:T(8,128)(2,1)} %all-to-all-done) | data formatting | bytes 8388608 | tf_op jit(solution)/shard_map/all_to_all | solution.py:147
  88.8 2.9 %copy.70 = bf16[1,4,16,4,64,128]{5,4,3,1,0,2:T(8,128)(2,1)} copy(bf16[1,4,16,4,64,128]{5,4,3,2,1,0:T(8,128)(2,1)S(1)} %bitcast.52) | data formatting | bytes 8388608 | tf_op jit(solution)/shard_map/all_to_all | solution.py:147
  91.8 5.8 %all-to-all-start.1 = ((bf16[1,4,16,4,64,128]{5,4,3,1,0,2:T(8,128)(2,1)}), bf16[1,4,16,4,64,128]{5,4,3,1,0,2:T(8,128)(2,1)}, u32[]{:S(2)}, u32[]{:S(2)}) async-start(bf16[1,4,16,4,64,128]{5,4,3,1,0,2:T(8,128)(2,1)} %copy.70), calls=%async_computation.1 | async-start | bytes 8388608 | tf_op jit(solution)/shard_map/all_to_all | solution.py:146
  97.6 18.3 %divide_convert_fusion = bf16[2,2048,128]{2,1,0:T(8,128)(2,1)S(1)} fusion(bf16[2048,2,128]{0,2,1:T(8,128)(2,1)} %bitcast.68, f32[2,2048,2048]{1,2,0:T(8,128)} %get-tuple-element.11, f32[2,2048]{1,0:T(2,128)S(1)} %broadcast_maximum_fusion, pred[2048,2048]{0,1:T(8,128)(4,1)} %broadcast_compare_fusion, f32[2,2048]{1,0:T(2,128)S(1)} %fusion.1), kind=kOutput, calls=%fused_computation.12 | convolution fusion | flops 2190475264 | bytes 39878656 | tf_op jit(solution)/shard_map/kqn,nkd->kqd/dot_general | solution.py:106
  115.9 0.7 copy.67
  116.6 1.2 copy.83
  117.8 27.1 %all-to-all-done.1 = bf16[1,4,16,4,64,128]{5,4,3,1,0,2:T(8,128)(2,1)} async-done(((bf16[1,4,16,4,64,128]{5,4,3,1,0,2:T(8,128)(2,1)}), bf16[1,4,16,4,64,128]{5,4,3,1,0,2:T(8,128)(2,1)}, u32[]{:S(2)}, u32[]{:S(2)}) %all-to-all-start.1) | async-done | bytes 4194336 | tf_op jit(solution)/shard_map/all_to_all | solution.py:146
  144.9 3.1 %copy.71 = bf16[1,4,16,4,64,128]{5,4,3,2,1,0:T(8,128)(2,1)S(1)} copy(bf16[1,4,16,4,64,128]{5,4,3,1,0,2:T(8,128)(2,1)} %all-to-all-done.1) | data formatting | bytes 8388608 | tf_op jit(solution)/shard_map/all_to_all | solution.py:146
  148.1 3.0 %copy.72 = bf16[2,1,4,8,4,64,128]{6,5,4,3,2,0,1:T(8,128)(2,1)} copy(bf16[2,1,4,8,4,64,128]{6,5,4,3,0,2,1:T(8,128)(2,1)S(1)} %bitcast.53) | data formatting | bytes 8388608 | tf_op jit(solution)/shard_map/all_to_all | solution.py:146
  (41 shorter events, 2.2 us)
Async XLA Ops:
  7.2 21.5 %copy-start = (bf16[256,1024]{1,0:T(8,128)(2,1)S(1)}, bf16[256,1024]{1,0:T(8,128)(2,1)}, u32[]{:S(2)}) copy-start(bf16[256,1024]{1,0:T(8,128)(2,1)} %param.13) | copy-start | bytes 1572868
  7.2 46.3 %all-gather.3.cloned.1.call-start = ((), (), s32[]{:S(2)}) async-start(), calls=%async_computation.2 | async-start | bytes 1179648 | tf_op jit(solution)/shard_map/all_gather | solution.py:89
  23.4 7.1 %copy-start.3 = (bf16[256,2048]{1,0:T(8,128)(2,1)S(1)}, bf16[256,2048]{1,0:T(8,128)(2,1)}, u32[]{:S(2)}) copy-start(bf16[256,2048]{1,0:T(8,128)(2,1)} %param.11) | copy-start | bytes 3145732
  23.4 62.2 %all-to-all-start = ((bf16[4,4,4,4,64,128]{5,4,3,2,1,0:T(8,128)(2,1)}), bf16[4,4,4,4,64,128]{5,4,3,2,1,0:T(8,128)(2,1)}, u32[]{:S(2)}, u32[]{:S(2)}) async-start(bf16[4,4,4,4,64,128]{5,4,3,2,1,0:T(8,128)(2,1)} %bitcast.51), calls=%async_computation | async-start | bytes 8388608 | tf_op jit(solution)/shard_map/all_to_all | solution.py:147
  28.4 69.2 %all-gather.5.cloned.1.call-start = ((), (), s32[]{:S(2)}) async-start(), calls=%async_computation.3 | async-start | bytes 1179648 | tf_op jit(solution)/shard_map/all_gather | solution.py:90
  28.7 2.5 %copy-start.5 = (f32[2048]{0:T(1024)S(1)}, f32[2048]{0:T(1024)}, u32[]{:S(2)}) copy-start(f32[2048]{0:T(1024)} %param.14) | copy-start | bytes 24580
  31.4 1.4 copy-start.4
  53.5 16.9 %copy-start.2 = (pred[2048,2048]{0,1:T(8,128)(4,1)S(1)}, pred[2048,2048]{0,1:T(8,128)(4,1)}, u32[]{:S(2)}) copy-start(pred[2048,2048]{0,1:T(8,128)(4,1)} %broadcast_compare_fusion) | copy-start | bytes 12582916
  91.8 53.2 %all-to-all-start.1 = ((bf16[1,4,16,4,64,128]{5,4,3,1,0,2:T(8,128)(2,1)}), bf16[1,4,16,4,64,128]{5,4,3,1,0,2:T(8,128)(2,1)}, u32[]{:S(2)}, u32[]{:S(2)}) async-start(bf16[1,4,16,4,64,128]{5,4,3,1,0,2:T(8,128)(2,1)} %copy.70), calls=%async_computation.1 | async-start | bytes 8388608 | tf_op jit(solution)/shard_map/all_to_all | solution.py:146
  148.1 3.0 %copy-start.1 = (bf16[256,1024]{1,0:T(8,128)(2,1)S(1)}, bf16[256,1024]{1,0:T(8,128)(2,1)}, u32[]{:S(2)}) copy-start(bf16[256,1024]{1,0:T(8,128)(2,1)} %param.13) | copy-start | bytes 1572868
Sparse Core Ops, SparseCore 0:
  11.2 42.2 all-gather.2
  55.5 38.4 all-gather.4
where the time goes:
time: 159 us; the launch traced here: 158 us
  waiting for transfers between devices  42.3 us (27%)
  matrix products  36.4 us (23%)
  other arithmetic  30.7 us (19%)
  local copies, waits for them, and re-layouts  23.1 us (15%)
  between operations  14.4 us (9%)
  starting transfers between devices  11.1 us (7%)
    all_to_all x1, waiting for transfers between devices, shards(): lax.all_to_all(lax.all_to_all(outgoing, 'dec', split_axis=0, concat_axis=...  27.1 us
    dot_general x1, matrix products, shards(): jnp.einsum('kqn,nkd->kqd', weights.astype(jnp.bfloat16), piece_values.res...  18.3 us
    dot_general x1, matrix products, shards(): jnp.einsum('kqd,nkd->kqn', query_rows, piece_keys.reshape(count, kv_local...  16.9 us
    reduce_sum x1, other arithmetic, shards(): total = jnp.sum(weights, axis=2)  15.2 us
    all_gather x1, waiting for transfers between devices, shards(): piece_keys = lax.all_gather(keys_rot, ('pre', 'rep'), axis=0, tiled=True)  15.1 us
    all_to_all x2, local copies, waits for them, and re-layouts, shards(): lax.all_to_all(lax.all_to_all(outgoing, 'dec', split_axis=0, concat_axis=...  6.13 us
    all_to_all x2, local copies, waits for them, and re-layouts, shards(): lax.all_to_all(outgoing, 'dec', split_axis=0, concat_axis=2, tiled=True)  6.08 us
    all_to_all x1, starting transfers between devices, shards(): lax.all_to_all(lax.all_to_all(outgoing, 'dec', split_axis=0, concat_axis=...  5.82 us
  transfers between devices with their start and end apart: 4, of which 2 were waited for; matrix products, arithmetic and copies ran while one was open for 51% of the time, Pallas kernels for 0%

commit v1 on v0

v1 whole, which is shorter than its diff:
```python
import functools

import jax
import jax.numpy as jnp
import numpy as np
from jax import lax
from jax.experimental import pallas as pl
from jax.experimental.pallas import tpu as pltpu
from jax.sharding import PartitionSpec as P

HEADS = 64
KVH = 8
HD = 128
BLOCK = 128

rope_base = 1000000.0
masked_score = -1e30
log2_e = 1.4426950408889634

ANY = pl.BlockSpec(memory_space=pl.ANY)
SMEM = pl.BlockSpec(memory_space=pltpu.SMEM)
VMEM = pl.BlockSpec(memory_space=pltpu.VMEM)
SMALL = pl.CostEstimate(flops=1, bytes_accessed=1, transcendentals=0)


def row_freqs():
    lane = np.arange(HD) % (HD // 2)
    freqs = 1.0 / rope_base ** (lane * (2.0 / HD))
    return jnp.asarray(freqs.astype(np.float32).reshape(1, HD))


def rotate(values, cosine, sine):
    return values * cosine + pltpu.roll(values, HD // 2, 1) * sine


def turn_kernel(
    dims,
    pos_ref,
    freq_ref,
    key_bias_ref,
    value_bias_ref,
    keys_hbm,
    values_hbm,
    kv_ref,
    cos_ref,
    sin_ref,
    qpos_ref,
    keys_buf,
    values_buf,
    sems,
):
    kv_local, head_count, rows, rep_size = dims
    pre, dec, rep = lax.axis_index("pre"), lax.axis_index("dec"), lax.axis_index("rep")
    kv_first = dec * head_count // (HEADS // KVH)
    columns = pl.ds(pl.multiple_of(kv_first * HD, HD), kv_local * HD)
    keys_in = pltpu.make_async_copy(keys_hbm.at[:, columns], keys_buf, sems.at[0])
    values_in = pltpu.make_async_copy(values_hbm.at[:, columns], values_buf, sems.at[1])
    keys_in.start()
    values_in.start()
    first = (pre * rep_size + rep) * (rows // HD)
    lanes = lax.broadcasted_iota(jnp.int32, (HD, HD), 1)
    for r in range(rows // HD):
        part = slice(r * HD, (r + 1) * HD)
        row = pos_ref[pl.ds(first + r, 1), :]
        column = jnp.broadcast_to(row, (HD, HD)).astype(jnp.float32).T
        qpos_ref[part, :] = column.astype(jnp.int32)
        angle = column * freq_ref[...]
        sine = jnp.sin(angle)
        cos_ref[part, :] = jnp.cos(angle)
        sin_ref[part, :] = jnp.where(lanes < HD // 2, -sine, sine)
    keys_in.wait()
    values_in.wait()
    for g in range(kv_local):
        where = pl.ds(pl.multiple_of((kv_first + g) * HD, HD), HD)
        part = slice(g * HD, (g + 1) * HD)
        shifted = keys_buf[:, part].astype(jnp.float32) + key_bias_ref[:, where]
        turned = rotate(shifted, cos_ref[...], sin_ref[...]).astype(jnp.bfloat16)
        biased = values_buf[:, part].astype(jnp.float32) + value_bias_ref[:, where]
        biased = biased.astype(jnp.bfloat16)
        kv_ref[0, g] = turned
        kv_ref[1, g] = biased


def turn(dims, positions, key_bias, value_bias, keys, values):
    kv_local, head_count, rows, rep_size = dims
    return pl.pallas_call(
        functools.partial(turn_kernel, dims),
        out_shape=[
            jax.ShapeDtypeStruct((2, kv_local, rows, HD), jnp.bfloat16),
            jax.ShapeDtypeStruct((rows, HD), jnp.float32),
            jax.ShapeDtypeStruct((rows, HD), jnp.float32),
            jax.ShapeDtypeStruct((rows, HD), jnp.int32),
        ],
        in_specs=[VMEM] * 4 + [ANY] * 2,
        out_specs=[VMEM] * 4,
        scratch_shapes=[
            pltpu.VMEM((rows, kv_local * HD), jnp.bfloat16),
            pltpu.VMEM((rows, kv_local * HD), jnp.bfloat16),
            pltpu.SemaphoreType.DMA((2,)),
        ],
        cost_estimate=SMALL,
        name="turn",
    )(
        positions.reshape(-1, HD),
        row_freqs(),
        key_bias.reshape(1, -1),
        value_bias.reshape(1, -1),
        keys,
        values,
    )


def pack_kernel(dims, page_ref, lengths_ref, replica_ref, kv_hbm, cache_hbm, *rest):
    blk_count, group, dec_size = dims
    sends = rest[:dec_size]
    held, valid, counts, in_sems, out_sems = rest[dec_size:]
    pre, dec, rep = lax.axis_index("pre"), lax.axis_index("dec"), lax.axis_index("rep")
    blocks_in = [
        pltpu.make_async_copy(cache_hbm.at[0, b], held.at[b], in_sems.at[b])
        for b in range(blk_count)
    ]
    for copy in blocks_in:
        copy.start()
    blocks_all = valid.shape[0]
    for k in range(blocks_all):
        valid[k] = 0
    for d in range(dec_size):
        counts[d] = 0

    def request(i, start):
        mine = replica_ref[i] == rep
        length = lengths_ref[i]
        number = jnp.where(mine, (length + (BLOCK - 1)) // BLOCK, 0)

        def block(k, carry):
            valid[start + k] = jnp.minimum(BLOCK, length - BLOCK * k)
            return carry

        lax.fori_loop(0, jnp.minimum(number, blocks_all - start), block, 0)
        return start + number

    lax.fori_loop(0, lengths_ref.shape[0], request, 0)
    place = pre * group + dec % group
    lane = lax.broadcasted_iota(jnp.int32, held.shape[1:], len(held.shape) - 2)
    for b in range(blk_count):
        k = pre * blk_count + b
        blocks_in[b].wait()
        limit = valid[k]

        @pl.when(limit < BLOCK)
        def _(b=b, limit=limit):
            held[b] = jnp.where(lane < limit, held[b], jnp.zeros_like(held[b]))

        target = page_ref[rep, k]
        rank = counts[target]
        counts[target] = rank + 1
        for j in range(dec_size):

            @pl.when(target == (place ^ j))
            def _(b=b, j=j, rank=rank):
                pltpu.make_async_copy(held.at[b], sends[j].at[rank], out_sems.at[b]).start()

    for b in range(blk_count):
        pltpu.make_async_copy(held.at[b], sends[0].at[0], out_sems.at[b]).wait()


def pack(dims, capacity, page_table, lengths, replica_of, kv, cache):
    blk_count, group, dec_size = dims
    block = cache.shape[2:]
    return pl.pallas_call(
        functools.partial(pack_kernel, dims),
        out_shape=[jax.ShapeDtypeStruct((capacity,) + block, jnp.bfloat16)] * dec_size,
        in_specs=[SMEM] * 3 + [ANY] * 2,
        out_specs=[ANY] * dec_size,
        scratch_shapes=[
            pltpu.VMEM((blk_count,) + block, jnp.bfloat16),
            pltpu.SMEM((page_table.shape[1],), jnp.int32),
            pltpu.SMEM((dec_size,), jnp.int32),
            pltpu.SemaphoreType.DMA((blk_count,)),
            pltpu.SemaphoreType.DMA((blk_count,)),
        ],
        cost_estimate=SMALL,
        name="pack",
    )(page_table, lengths, replica_of, kv, cache)


def after(value, *before):
    return lax.optimization_barrier((value,) + before)[0] if before else value


def query_kernel(query_ref, bias_ref, cos_ref, sin_ref, out_ref):
    for h in range(out_ref.shape[0]):
        columns = slice(h * HD, (h + 1) * HD)
        shifted = query_ref[:, columns].astype(jnp.float32) + bias_ref[:, columns]
        out_ref[h] = rotate(shifted, cos_ref[...], sin_ref[...]).astype(jnp.bfloat16)


def rotate_queries(queries, bias, cosine, sine):
    rows, columns = queries.shape
    return pl.pallas_call(
        query_kernel,
        out_shape=jax.ShapeDtypeStruct((columns // HD, rows, HD), jnp.bfloat16),
        in_specs=[VMEM] * 4,
        out_specs=VMEM,
        cost_estimate=SMALL,
        name="rotate_queries",
    )(queries, bias.reshape(1, -1), cosine, sine)


def attend_kernel(moves, rep_size, first, last, query_ref, qpos_ref, pos_ref, *rest):
    chunks, rest = rest[: len(moves)], rest[len(moves) :]
    if not first:
        stat_in, sum_in, rest = rest[0], rest[1], rest[2:]
    outs = rest
    step_heads, rows, _ = query_ref.shape
    half = HD // 2
    pre, rep = lax.axis_index("pre"), lax.axis_index("rep")
    scale = HD ** (-0.5) * log2_e
    qpos = qpos_ref[:, :1]
    lanes = lax.broadcasted_iota(jnp.int32, (rows, HD), 1)
    bias, keys, values = [], [], []
    for (move_pre, move_rep), chunk in zip(moves, chunks):
        block = (pre ^ move_pre) * rep_size + (rep ^ move_rep)
        parts = [pos_ref[pl.ds(block * (rows // HD) + r, 1), :] for r in range(rows // HD)]
        bias.append(jnp.concatenate(parts, axis=1) <= qpos)
        keys.append(chunk[0, 0])
        values.append(jnp.concatenate([chunk[1, 0], jnp.ones((rows, HD), jnp.bfloat16)], axis=1))
    stat = jnp.zeros((rows, HD), jnp.float32)
    for h in range(step_heads):
        query = query_ref[h]
        scores = []
        for allowed, key in zip(bias, keys):
            product = lax.dot_general(
                query, key, (((1,), (1,)), ((), ())), preferred_element_type=jnp.float32
            )
            scores.append(jnp.where(allowed, product, masked_score))
        newest = jnp.max(functools.reduce(jnp.maximum, scores), axis=1, keepdims=True)
        if not first:
            best = stat_in[0, :, h : h + 1]
            newest = jnp.maximum(newest, best)
            decay = jnp.exp2((best - newest) * scale)
        both = 0.0
        for score, value in zip(scores, values):
            weights = jnp.exp2((score - newest) * scale)
            both = both + jnp.dot(
                weights.astype(jnp.bfloat16), value, preferred_element_type=jnp.float32
            )
        added, total = both[:, :HD], both[:, HD:]
        if not first:
            total = total + stat_in[0, :, half + h : half + h + 1] * decay
            added = added + sum_in[h] * decay
        if last:
            outs[0][:, h * HD : (h + 1) * HD] = (added / total).astype(jnp.bfloat16)
        else:
            stat = jnp.where(lanes == h, newest, jnp.where(lanes == half + h, total, stat))
            outs[1][h] = added
    if not last:
        outs[0][0] = stat


def attend(pairs, rep_size, per_group, queries, qpos, positions, state, last):
    heads, rows, _ = queries.shape
    step_heads = per_group
    first = state is None
    moves, chunks = zip(*pairs)
    whole = lambda i: (0, 0)
    by_head = pl.BlockSpec((step_heads, rows, HD), lambda i: (i, 0, 0))
    by_step = pl.BlockSpec((1, rows, HD), lambda i: (i, 0, 0))
    chunk_spec = pl.BlockSpec((2, 1, rows, HD), lambda i: (0, i, 0, 0))
    pos2 = positions.reshape(-1, HD)
    in_specs = (
        [by_head, pl.BlockSpec((rows, HD), whole), pl.BlockSpec(pos2.shape, whole)]
        + [chunk_spec] * len(chunks)
        + ([] if first else [by_step, by_head])
    )
    if last:
        out_shape = jax.ShapeDtypeStruct((rows, heads * HD), jnp.bfloat16)
        out_specs = pl.BlockSpec((rows, step_heads * HD), lambda i: (0, i))
    else:
        out_shape = [
            jax.ShapeDtypeStruct((heads // step_heads, rows, HD), jnp.float32),
            jax.ShapeDtypeStruct((heads, rows, HD), jnp.float32),
        ]
        out_specs = [by_step, by_head]
    return pl.pallas_call(
        functools.partial(attend_kernel, moves, rep_size, first, last),
        grid=(heads // step_heads,),
        out_shape=out_shape,
        in_specs=in_specs,
        out_specs=out_specs,
        compiler_params=pltpu.CompilerParams(vmem_limit_bytes=40 << 20),
        cost_estimate=SMALL,
        name="attend",
    )(queries, qpos, pos2, *chunks, *(() if first else state))


def place_kernel(dims, here, rest_j, page_ref, own_hbm, *rest):
    blk_count, capacity, hl, group = dims
    arrived, rest = rest[: len(here)], rest[len(here) :]
    out_hbm, held, zeros, in_sems, out_sems = rest[-5:]
    pre, dec, rep = lax.axis_index("pre"), lax.axis_index("dec"), lax.axis_index("rep")

    def goal(j):
        source = dec ^ j
        run, part = source // group, source % group
        used = functools.reduce(
            jnp.logical_or,
            [page_ref[rep, run * blk_count + b] == dec for b in range(blk_count)],
        )
        return used, lambda c: out_hbm.at[0, 0, run * capacity + c, pl.ds(part * hl, hl)]

    moves = []
    for n, j in enumerate(here):
        used, to = goal(j)
        for c in range(capacity):
            inward = pltpu.make_async_copy(arrived[n].at[c], held.at[n, c], in_sems.at[n, c])
            outward = pltpu.make_async_copy(held.at[n, c], to(c), out_sems.at[n, c])
            moves.append((used, inward, outward))
            local = used & (dec // group == pre) if j == 0 else None
            if j == 0:
                kept = pltpu.make_async_copy(own_hbm.at[c], held.at[n, c], in_sems.at[n, c])

                @pl.when(local)
                def _(kept=kept):
                    kept.start()

            @pl.when(used if local is None else used & jnp.logical_not(local))
            def _(inward=inward):
                inward.start()

    fills = []
    if rest_j:
        zeros[...] = jnp.zeros_like(zeros)
        for n, j in enumerate(rest_j):
            used, to = goal(j)
            for c in range(capacity):
                fill = pltpu.make_async_copy(zeros, to(c), out_sems.at[len(here) + n, c])
                fills.append((used, fill))

                @pl.when(jnp.logical_not(used))
                def _(fill=fill):
                    fill.start()

    for used, inward, outward in moves:

        @pl.when(used)
        def _(inward=inward, outward=outward):
            inward.wait()
            outward.start()

    for used, inward, outward in moves:

        @pl.when(used)
        def _(outward=outward):
            outward.wait()

    for used, fill in fills:

        @pl.when(jnp.logical_not(used))
        def _(fill=fill):
            fill.wait()


def place(dims, pre_size, here, rest_j, page_table, own, arrived, buffer):
    blk_count, capacity, hl, group = dims
    block = arrived[0].shape[2:]
    count = len(here)
    kept = [] if buffer is None else [buffer]
    return pl.pallas_call(
        functools.partial(place_kernel, dims, here, rest_j),
        out_shape=jax.ShapeDtypeStruct((1, 1, pre_size * capacity, group * hl) + block, jnp.bfloat16),
        in_specs=[SMEM] + [ANY] * (1 + count + len(kept)),
        out_specs=ANY,
        scratch_shapes=[
            pltpu.VMEM((count, capacity, hl) + block, jnp.bfloat16),
            pltpu.VMEM((hl,) + block, jnp.bfloat16),
            pltpu.SemaphoreType.DMA((count, capacity)),
            pltpu.SemaphoreType.DMA((count + len(rest_j), capacity)),
        ],
        input_output_aliases={2 + count: 0} if kept else {},
        cost_estimate=SMALL,
        name="place",
    )(page_table, own, *arrived, *kept)


def shards(
    layer_queries,
    layer_keys,
    layer_values,
    query_bias,
    key_bias,
    value_bias,
    positions,
    lengths,
    replica_of,
    page_table,
    prefill_cache,
):
    pre_size, dec_size, rep_size = (lax.axis_size(a) for a in ("pre", "dec", "rep"))
    rows = layer_queries.shape[0]
    head_count = layer_queries.shape[1] // HD
    group_size = HEADS // KVH
    kv_local = max(1, head_count // group_size)
    per_group = head_count // kv_local
    blk_count, hl = prefill_cache.shape[1], prefill_cache.shape[2]
    capacity = 2 * blk_count // dec_size
    group = dec_size // pre_size
    kv, cosine, sine, qpos = turn(
        (kv_local, head_count, rows, rep_size), positions, key_bias, value_bias,
        layer_keys, layer_values,
    )
    sends = pack((blk_count, group, dec_size), capacity, page_table, lengths, replica_of, kv, prefill_cache)
    swap = lambda value, axis, size, hop: lax.ppermute(
        value, axis, [(i, i ^ hop) for i in range(size)]
    )
    near = [kv] + [swap(kv, "pre", pre_size, s) for s in range(1, pre_size)]
    arrived = {}

    def hand_over(j, *before):
        route = []
        for p in range(pre_size):
            for d in range(dec_size):
                goal = (p * group + d % group) ^ j
                pair = (p * dec_size + d, (d // group) * dec_size + goal)
                if pair[0] != pair[1]:
                    route.append(pair)
        arrived[j] = lax.ppermute(after(sends[j], *before), ("pre", "dec"), route)

    order = sorted(range(dec_size), key=lambda j: (j % group, j // group))
    attends = functools.partial(attend, rep_size=rep_size, per_group=per_group, qpos=qpos, positions=positions)
    hops = [1] + list(range(rep_size - 1, 1, -1))
    own = {r: swap(kv, "rep", rep_size, r) for r in hops}
    for j in order[:2]:
        hand_over(j, near[-1])
    for j in order[2:3]:
        hand_over(j, near[-1], own[1], own[hops[1]])
    queries = rotate_queries(layer_queries, query_bias, cosine, sine)
    state = attends([((s, 0), near[s]) for s in range(pre_size)], queries=queries, state=None, last=False)
    far = []
    for r in hops[1:]:
        for s in range(1, pre_size):
            wait = (own[r], state[0]) if r == hops[1] else (own[r], arrived[order[0]])
            far.append(((s, r), swap(after(near[s], *wait), "rep", rep_size, r)))
    for j in order[3:]:
        hand_over(j, near[-1], state[0], own[hops[-1]])
    state = attends([((0, r), own[r]) for r in hops], queries=queries, state=state, last=False)
    for s in range(1, pre_size):
        far.append(((s, 1), swap(after(near[s], state[0], arrived[order[1]]), "rep", rep_size, 1)))
    state = attends(far, queries=queries, state=state, last=True)
    split = dec_size // 2
    arrange = functools.partial(place, (blk_count, capacity, hl, group), pre_size)
    got = [arrived[j] for j in order]
    decode_cache = arrange(order[:split], order, page_table, sends[0], got[:split], None)
    decode_cache = arrange(order[split:], [], page_table, sends[0], got[split:], decode_cache)
    return (state, decode_cache)


def solution(mesh):
    placed = (
        P(("pre", "rep"), "dec"),
        P(("pre", "rep"), None),
        P(("pre", "rep"), None),
        P("dec"),
        P(),
        P(),
        P(),
        P(),
        P(),
        P(),
        P("rep", "pre", "dec", None, None, None),
    )
    return jax.shard_map(
        shards,
        mesh=mesh,
        in_specs=placed,
        out_specs=(P(("pre", "rep"), "dec"), P("rep", "dec", None, "pre", None, None, None)),
        check_vma=False,
    )
```

time: 159 us -> 74.5 us (0.47)
  matrix products: 36.4 us -> 0 us
  Pallas kernels: 0 us -> 34.8 us
  other arithmetic: 30.7 us -> 0 us
  waiting for transfers between devices: 42.3 us -> 12.8 us
  local copies, waits for them, and re-layouts: 23.1 us -> 5.32 us
  between operations: 14.4 us -> 0.79 us
  starting transfers between devices: 11.1 us -> 20.1 us
    dot_general x3 -> x0, matrix products: 36.4 us -> none  [the longest x1 18.3 us: shards(): jnp.einsum('kqn,nkd->kqd', weights.astype(jnp.bfloat16), piece_values.res...]
    pallas_call x0 -> x8, Pallas kernels: none -> 34.8 us  [the longest x3 19.8 us: attend(): pl.pallas_call(functools.partial(attend_kernel, moves, rep_size, first, l...]
    all_to_all x2 -> x0, waiting for transfers between devices: 27.1 us -> none  [the longest x1 27.1 us: shards(): lax.all_to_all(lax.all_to_all(outgoing, 'dec', split_axis=0, concat_axis=...]
    ppermute x0 -> x11, starting transfers between devices: none -> 20.1 us  [the longest x7 14.3 us: shards(): lax.ppermute(value, axis, [(i, i ^ hop) for i in range(size)])]
    reduce_sum x3 -> x0, other arithmetic: 16.3 us -> none  [the longest x1 15.2 us: shards(): total = jnp.sum(weights, axis=2)]
    all_gather x2 -> x0, waiting for transfers between devices: 15.1 us -> none  [the longest x1 15.1 us: shards(): piece_keys = lax.all_gather(keys_rot, ('pre', 'rep'), axis=0, tiled=True)]
    ppermute x0 -> x11, waiting for transfers between devices: none -> 12.8 us  [the longest x4 10.7 us: hand_over(): arrived[j] = lax.ppermute(after(sends[j], *before), ('pre', 'dec'), route)]
    all_to_all x4 -> x0, local copies, waits for them, and re-layouts: 12.2 us -> none  [the longest x2 6.13 us: shards(): lax.all_to_all(lax.all_to_all(outgoing, 'dec', split_axis=0, concat_axis=...]
  transfers between devices with their start and end apart: 4 -> 11, of which waited for: 2 -> 3; matrix products, arithmetic and copies ran while one was open for 51% -> 0% of each run, Pallas kernels for 0% -> 32%
where the time goes in v1:
time: 74.5 us; the launch traced here: 73.8 us
  Pallas kernels  34.8 us (47%)
  starting transfers between devices  20.1 us (27%)
  waiting for transfers between devices  12.8 us (17%)
  local copies, waits for them, and re-layouts  5.32 us (7%)
  between operations  0.79 us (1%)
    pallas_call x3, Pallas kernels, attend(): pl.pallas_call(functools.partial(attend_kernel, moves, rep_size, first, l...  19.8 us
    ppermute x7, starting transfers between devices, shards(): lax.ppermute(value, axis, [(i, i ^ hop) for i in range(size)])  14.3 us
    ppermute x4, waiting for transfers between devices, hand_over(): arrived[j] = lax.ppermute(after(sends[j], *before), ('pre', 'dec'), route)  10.7 us
    pallas_call x2, Pallas kernels, place(): pl.pallas_call(functools.partial(place_kernel, dims, here, rest_j), out_s...  6.4 us
    ppermute x4, starting transfers between devices, hand_over(): arrived[j] = lax.ppermute(after(sends[j], *before), ('pre', 'dec'), route)  5.81 us
    unnamed x22, local copies, waits for them, and re-layouts  5.32 us
    pallas_call x1, Pallas kernels, pack(): pl.pallas_call(functools.partial(pack_kernel, dims), out_shape=[jax.Shape...  3.17 us
    pallas_call x1, Pallas kernels, rotate_queries(): pl.pallas_call(query_kernel, out_shape=jax.ShapeDtypeStruct((columns // H...  2.86 us
  transfers between devices with their start and end apart: 11, of which 3 were waited for; matrix products, arithmetic and copies ran while one was open for 0% of the time, Pallas kernels for 32%

profile of v1, /device:TPU:0, one launch (start us, length us, event | category | flops | bytes accessed | tf_op | source)
XLA Modules:
  0.0 73.8 jit_solution(2703447699427887611)
XLA Ops:
  0.6 2.6 %turn.1 = (bf16[2,2,256,128]{3,2,1,0:T(8,128)(2,1)}, f32[256,128]{1,0:T(8,128)}, f32[256,128]{1,0:T(8,128)}, s32[256,128]{1,0:T(8,128)}) custom-call(s32[16,128]{1,0:T(8,128)} %bitcast.4, f32[1,128]{1,0:T(1,128)} %constant.2.clone.freq_ref, f32[1,1024]{1,0:T(1,128)} %bitcast.9, f32[1,1024]{1,0:T(1,128)} %bitcast.10, bf16[256,1024]{1,0:T(8,128)(2,1)} %keys_hbm.1, ...), custom_call_target="tpu_custom_call" | custom-call | flops 1 | bytes 1 | tf_op jit(solution)/shard_map/turn/pallas_call | solution.py:86
  3.3 0.0 copy-start.10
  3.3 3.0 %collective-permute-start = (bf16[2,2,256,128]{3,2,1,0:T(8,128)(2,1)}, bf16[2,2,256,128]{3,2,1,0:T(8,128)(2,1)}, u32[]{:S(2)}, u32[]{:S(2)}) collective-permute-start(bf16[2,2,256,128]{3,2,1,0:T(8,128)(2,1)} %get-tuple-element.24.rest_0_.kv_hbm), channel_id=1, source_target_pairs={{0,16},{16,0},{1,17},{17,1},{2,18},{18,2},{3,19},{19,3},{4,20},{20... | collective-permute-start | bytes 786440 | tf_op jit(solution)/shard_map/ppermute | solution.py:413
  6.3 1.6 %collective-permute-start.6 = (bf16[2,2,256,128]{3,2,1,0:T(8,128)(2,1)}, bf16[2,2,256,128]{3,2,1,0:T(8,128)(2,1)S(1)}, u32[]{:S(2)}, u32[]{:S(2)}) collective-permute-start(bf16[2,2,256,128]{3,2,1,0:T(8,128)(2,1)} %get-tuple-element.24.rest_0_.kv_hbm), channel_id=1, source_target_pairs={{0,1},{1,0},{2,3},{3,2},{4,5},{5,4},{6,7},{7,6},{8,9},{9,8},{10,11... | collective-permute-start | bytes 786440 | tf_op jit(solution)/shard_map/ppermute | solution.py:413
  7.9 2.6 %collective-permute-start.3 = (bf16[2,2,256,128]{3,2,1,0:T(8,128)(2,1)}, bf16[2,2,256,128]{3,2,1,0:T(8,128)(2,1)S(1)}, u32[]{:S(2)}, u32[]{:S(2)}) collective-permute-start(bf16[2,2,256,128]{3,2,1,0:T(8,128)(2,1)} %get-tuple-element.24.rest_0_.kv_hbm), channel_id=1, source_target_pairs={{0,2},{1,3},{2,0},{3,1},{4,6},{5,7},{6,4},{7,5},{8,10},{9,11},{10,... | collective-permute-start | bytes 786440 | tf_op jit(solution)/shard_map/ppermute | solution.py:413
  10.5 0.2 collective-permute-start.1
  10.7 3.2 %pack.1 = (bf16[4,4,4,64,128]{4,3,2,1,0:T(8,128)(2,1)}, bf16[4,4,4,64,128]{4,3,2,1,0:T(8,128)(2,1)}, bf16[4,4,4,64,128]{4,3,2,1,0:T(8,128)(2,1)}, bf16[4,4,4,64,128]{4,3,2,1,0:T(8,128)(2,1)}) custom-call(s32[4,16]{1,0:T(4,128)} %page_ref.5, s32[32]{0:T(128)} %lengths_ref.1, s32[32]{0:T(128)} %replica_ref.1, ...), custom_call_target="tpu_custom_call" | custom-call | flops 1 | bytes 1 | tf_op jit(solution)/shard_map/pack/pallas_call | solution.py:170
  13.9 0.0 collective-permute-done.rest_1_
  13.9 1.6 %collective-permute-start.4 = (bf16[4,4,4,64,128]{4,3,2,1,0:T(8,128)(2,1)}, bf16[4,4,4,64,128]{4,3,2,1,0:T(8,128)(2,1)}, u32[]{:S(2)}, u32[]{:S(2)}) collective-permute-start(bf16[4,4,4,64,128]{4,3,2,1,0:T(8,128)(2,1)} %get-tuple-element.28.own_hbm), channel_id=1, source_target_pairs={{8,16},{12,20},{16,8},{20,12},{9,17},{13,21},{17,9},{21,13},{10,18... | collective-permute-start | bytes 3145736 | tf_op jit(solution)/shard_map/ppermute | solution.py:427
  15.5 2.6 %collective-permute-start.7 = (bf16[4,4,4,64,128]{4,3,2,1,0:T(8,128)(2,1)}, bf16[4,4,4,64,128]{4,3,2,1,0:T(8,128)(2,1)}, u32[]{:S(2)}, u32[]{:S(2)}) collective-permute-start(bf16[4,4,4,64,128]{4,3,2,1,0:T(8,128)(2,1)} %get-tuple-element.33), channel_id=1, source_target_pairs={{0,8},{4,12},{8,24},{12,28},{16,0},{20,4},{24,16},{28,20},{1,9},{5... | collective-permute-start | bytes 3145736 | tf_op jit(solution)/shard_map/ppermute | solution.py:427
  18.1 2.9 %rotate_queries.1.query_ref = bf16[16,256,128]{2,1,0:T(8,128)(2,1)} custom-call(bf16[256,2048]{1,0:T(8,128)(2,1)} %query_ref.1, f32[1,2048]{1,0:T(1,128)} %bitcast.8, f32[256,128]{1,0:T(8,128)} %get-tuple-element.21.cos_ref, f32[256,128]{1,0:T(8,128)} %get-tuple-element.22.sin_ref), custom_call_target="tpu_custom_call" | custom-call | flops 1 | bytes 1 | tf_op jit(solution)/shard_map/rotate_queries/pallas_call | solution.py:200
  21.0 0.0 copy-start
  21.0 1.2 %copy-done = bf16[16,256,128]{2,1,0:T(8,128)(2,1)S(1)} copy-done((bf16[16,256,128]{2,1,0:T(8,128)(2,1)S(1)}, bf16[16,256,128]{2,1,0:T(8,128)(2,1)}, u32[]{:S(2)}) %copy-start) | copy-done | bytes 1048600
  22.2 4.4 %attend.3 = (f32[2,256,128]{2,1,0:T(8,128)S(1)}, f32[16,256,128]{2,1,0:T(8,128)S(1)}) custom-call(bf16[16,256,128]{2,1,0:T(8,128)(2,1)S(1)} %copy-done, s32[256,128]{1,0:T(8,128)S(1)} %copy-done.2, s32[16,128]{1,0:T(8,128)S(1)} %bitcast.5, bf16[2,2,256,128]{3,2,1,0:T(8,128)(2,1)S(1)} %copy-done.3, bf16[2,2,256,128]{3,2,1,0:T(8,128)(2,1)} %collective-permute-done.rest_1_), custom_call_target="tpu_custom_call" | custom-call | flops 1 | bytes 1 | tf_op jit(solution)/shard_map/attend/pallas_call | solution.py:285
  26.6 1.0 %collective-permute-done.1.rest_1_ = bf16[2,2,256,128]{3,2,1,0:T(8,128)(2,1)S(1)} collective-permute-done((bf16[2,2,256,128]{3,2,1,0:T(8,128)(2,1)}, bf16[2,2,256,128]{3,2,1,0:T(8,128)(2,1)S(1)}, u32[]{:S(2)}, u32[]{:S(2)}) %collective-permute-start.1) | collective-permute-done | bytes 262176 | tf_op jit(solution)/shard_map/ppermute | solution.py:413
  27.6 0.7 %copy-done.6 = bf16[2,2,256,128]{3,2,1,0:T(8,128)(2,1)} copy-done((bf16[2,2,256,128]{3,2,1,0:T(8,128)(2,1)}, bf16[2,2,256,128]{3,2,1,0:T(8,128)(2,1)S(1)}, u32[]{:S(2)}) %copy-start.6) | copy-done | bytes 262168
  28.4 1.1 %collective-permute-done.3.rest_2_ = bf16[2,2,256,128]{3,2,1,0:T(8,128)(2,1)S(1)} collective-permute-done((bf16[2,2,256,128]{3,2,1,0:T(8,128)(2,1)}, bf16[2,2,256,128]{3,2,1,0:T(8,128)(2,1)S(1)}, u32[]{:S(2)}, u32[]{:S(2)}) %collective-permute-start.3) | collective-permute-done | bytes 262176 | tf_op jit(solution)/shard_map/ppermute | solution.py:413
  29.5 0.7 copy-done.4
  30.2 1.6 %collective-permute-start.9 = (bf16[4,4,4,64,128]{4,3,2,1,0:T(8,128)(2,1)}, bf16[4,4,4,64,128]{4,3,2,1,0:T(8,128)(2,1)}, u32[]{:S(2)}, u32[]{:S(2)}) collective-permute-start(bf16[4,4,4,64,128]{4,3,2,1,0:T(8,128)(2,1)} %get-tuple-element.37), channel_id=1, source_target_pairs={{0,4},{4,0},{8,20},{12,16},{16,12},{20,8},{24,28},{28,24},{1,5},{5... | collective-permute-start | bytes 3145736 | tf_op jit(solution)/shard_map/ppermute | solution.py:427
  31.8 2.5 %collective-permute-start.2 = (bf16[2,2,256,128]{3,2,1,0:T(8,128)(2,1)}, bf16[2,2,256,128]{3,2,1,0:T(8,128)(2,1)}, u32[]{:S(2)}, u32[]{:S(2)}) collective-permute-start(bf16[2,2,256,128]{3,2,1,0:T(8,128)(2,1)} %collective-permute-done.rest_1_), channel_id=1, source_target_pairs={{0,3},{1,2},{2,1},{3,0},{4,7},{5,6},{6,5},{7,4},{8,11},{9,10},{10,... | collective-permute-start | bytes 786440 | tf_op jit(solution)/shard_map/ppermute | solution.py:413
  34.3 0.9 %copy-done.5 = bf16[2,2,256,128]{3,2,1,0:T(8,128)(2,1)S(1)} copy-done((bf16[2,2,256,128]{3,2,1,0:T(8,128)(2,1)S(1)}, bf16[2,2,256,128]{3,2,1,0:T(8,128)(2,1)}, u32[]{:S(2)}) %copy-start.5) | copy-done | bytes 262168
  35.2 0.9 %copy-done.7 = bf16[2,2,256,128]{3,2,1,0:T(8,128)(2,1)S(1)} copy-done((bf16[2,2,256,128]{3,2,1,0:T(8,128)(2,1)S(1)}, bf16[2,2,256,128]{3,2,1,0:T(8,128)(2,1)}, u32[]{:S(2)}) %copy-start.7) | copy-done | bytes 262168
  36.2 6.9 %attend.4 = (f32[2,256,128]{2,1,0:T(8,128)S(1)}, f32[16,256,128]{2,1,0:T(8,128)S(1)}) custom-call(bf16[16,256,128]{2,1,0:T(8,128)(2,1)S(1)} %copy-done.1, s32[256,128]{1,0:T(8,128)S(1)} %copy-done.2, s32[16,128]{1,0:T(8,128)S(1)} %bitcast.6, bf16[2,2,256,128]{3,2,1,0:T(8,128)(2,1)S(1)} %collective-permute-done.6.rest_0_, ...), custom_call_target="tpu_custom_call" | custom-call | flops 1 | bytes 1 | tf_op jit(solution)/shard_map/attend/pallas_call | solution.py:285
  43.1 0.0 copy-start.8
  43.1 0.7 copy-done.8
  43.8 4.2 %collective-permute-start.5 = (bf16[2,2,256,128]{3,2,1,0:T(8,128)(2,1)}, bf16[2,2,256,128]{3,2,1,0:T(8,128)(2,1)}, u32[]{:S(2)}, u32[]{:S(2)}) collective-permute-start(bf16[2,2,256,128]{3,2,1,0:T(8,128)(2,1)} %collective-permute-done.rest_1_), channel_id=1, source_target_pairs={{0,2},{1,3},{2,0},{3,1},{4,6},{5,7},{6,4},{7,5},{8,10},{9,11},{10,... | collective-permute-start | bytes 786440 | tf_op jit(solution)/shard_map/ppermute | solution.py:413
  48.0 0.2 collective-permute-start.8
  48.2 3.3 %place.2.rest_2_ = bf16[1,1,8,8,4,64,128]{6,5,4,3,2,1,0:T(8,128)(2,1)} custom-call(s32[4,16]{1,0:T(4,128)} %page_ref.5, bf16[4,4,4,64,128]{4,3,2,1,0:T(8,128)(2,1)} %get-tuple-element.28.own_hbm, bf16[4,4,4,64,128]{4,3,2,1,0:T(8,128)(2,1)} %collective-permute-done.4.rest_0_, bf16[4,4,4,64,128]{4,3,2,1,0:T(8,128)(2,1)} %collective-permute-done.7.rest_1_), custom_call_target="tpu_custom_call" | custom-call | flops 1 | bytes 1 | tf_op jit(solution)/shard_map/place/pallas_call | solution.py:369
  51.5 0.0 copy-start.9
  51.5 10.7 %collective-permute-done.10.rest_1_ = bf16[4,4,4,64,128]{4,3,2,1,0:T(8,128)(2,1)} collective-permute-done((bf16[4,4,4,64,128]{4,3,2,1,0:T(8,128)(2,1)}, bf16[4,4,4,64,128]{4,3,2,1,0:T(8,128)(2,1)}, u32[]{:S(2)}, u32[]{:S(2)}) %collective-permute-start.10) | collective-permute-done | bytes 1048608 | tf_op jit(solution)/shard_map/ppermute | solution.py:427
  62.1 3.1 %place.3 = bf16[1,1,8,8,4,64,128]{6,5,4,3,2,1,0:T(8,128)(2,1)} custom-call(s32[4,16]{1,0:T(4,128)} %page_ref.5, bf16[4,4,4,64,128]{4,3,2,1,0:T(8,128)(2,1)} %get-tuple-element.28.own_hbm, bf16[4,4,4,64,128]{4,3,2,1,0:T(8,128)(2,1)} %collective-permute-done.9.rest_0_, ...), custom_call_target="tpu_custom_call", output_to_operand_aliasing={{}: (4, {})} | custom-call | flops 1 | bytes 1 | tf_op jit(solution)/shard_map/place/pallas_call | solution.py:369
  65.3 8.5 %attend.5 = bf16[256,2048]{1,0:T(8,128)(2,1)} custom-call(bf16[16,256,128]{2,1,0:T(8,128)(2,1)S(1)} %copy-done.1, s32[256,128]{1,0:T(8,128)S(1)} %copy-done.2, s32[16,128]{1,0:T(8,128)S(1)} %bitcast.7, bf16[2,2,256,128]{3,2,1,0:T(8,128)(2,1)} %collective-permute-done.2.rest_0_, bf16[2,2,256,128]{3,2,1,0:T(8,128)(2,1)} %collective-permute-done.5.rest_1_, ...), custom_call_target="tpu_custom_call" | custom-call | flops 1 | bytes 1 | tf_op jit(solution)/shard_map/attend/pallas_call | solution.py:285
  (20 shorter events, 0.0 us)
Async XLA Ops:
  3.2 17.7 %copy-start.2 = (s32[256,128]{1,0:T(8,128)S(1)}, s32[256,128]{1,0:T(8,128)}, u32[]{:S(2)}) copy-start(s32[256,128]{1,0:T(8,128)} %get-tuple-element.23.qpos_ref) | copy-start | bytes 393220
  3.2 17.7 %copy-start.3 = (bf16[2,2,256,128]{3,2,1,0:T(8,128)(2,1)S(1)}, bf16[2,2,256,128]{3,2,1,0:T(8,128)(2,1)}, u32[]{:S(2)}) copy-start(bf16[2,2,256,128]{3,2,1,0:T(8,128)(2,1)} %get-tuple-element.24.rest_0_.kv_hbm) | copy-start | bytes 786436
  3.3 17.7 %copy-start.10 = (s32[2048]{0:T(1024)S(1)}, s32[2048]{0:T(1024)}, u32[]{:S(2)}) copy-start(s32[2048]{0:T(1024)} %param.18) | copy-start | bytes 24580
  3.3 10.6 %collective-permute-start = (bf16[2,2,256,128]{3,2,1,0:T(8,128)(2,1)}, bf16[2,2,256,128]{3,2,1,0:T(8,128)(2,1)}, u32[]{:S(2)}, u32[]{:S(2)}) collective-permute-start(bf16[2,2,256,128]{3,2,1,0:T(8,128)(2,1)} %get-tuple-element.24.rest_0_.kv_hbm), channel_id=1, source_target_pairs={{0,16},{16,0},{1,17},{17,1},{2,18},{18,2},{3,19},{19,3},{4,20},{20... | collective-permute-start | bytes 786440 | tf_op jit(solution)/shard_map/ppermute | solution.py:413
  6.3 20.3 %collective-permute-start.6 = (bf16[2,2,256,128]{3,2,1,0:T(8,128)(2,1)}, bf16[2,2,256,128]{3,2,1,0:T(8,128)(2,1)S(1)}, u32[]{:S(2)}, u32[]{:S(2)}) collective-permute-start(bf16[2,2,256,128]{3,2,1,0:T(8,128)(2,1)} %get-tuple-element.24.rest_0_.kv_hbm), channel_id=1, source_target_pairs={{0,1},{1,0},{2,3},{3,2},{4,5},{5,4},{6,7},{7,6},{8,9},{9,8},{10,11... | collective-permute-start | bytes 786440 | tf_op jit(solution)/shard_map/ppermute | solution.py:413
  7.9 21.6 %collective-permute-start.3 = (bf16[2,2,256,128]{3,2,1,0:T(8,128)(2,1)}, bf16[2,2,256,128]{3,2,1,0:T(8,128)(2,1)S(1)}, u32[]{:S(2)}, u32[]{:S(2)}) collective-permute-start(bf16[2,2,256,128]{3,2,1,0:T(8,128)(2,1)} %get-tuple-element.24.rest_0_.kv_hbm), channel_id=1, source_target_pairs={{0,2},{1,3},{2,0},{3,1},{4,6},{5,7},{6,4},{7,5},{8,10},{9,11},{10,... | collective-permute-start | bytes 786440 | tf_op jit(solution)/shard_map/ppermute | solution.py:413
  10.5 17.2 %collective-permute-start.1 = (bf16[2,2,256,128]{3,2,1,0:T(8,128)(2,1)}, bf16[2,2,256,128]{3,2,1,0:T(8,128)(2,1)S(1)}, u32[]{:S(2)}, u32[]{:S(2)}) collective-permute-start(bf16[2,2,256,128]{3,2,1,0:T(8,128)(2,1)} %get-tuple-element.24.rest_0_.kv_hbm), channel_id=1, source_target_pairs={{0,3},{1,2},{2,1},{3,0},{4,7},{5,6},{6,5},{7,4},{8,11},{9,10},{10,... | collective-permute-start | bytes 786440 | tf_op jit(solution)/shard_map/ppermute | solution.py:413
  13.9 29.9 %collective-permute-start.4 = (bf16[4,4,4,64,128]{4,3,2,1,0:T(8,128)(2,1)}, bf16[4,4,4,64,128]{4,3,2,1,0:T(8,128)(2,1)}, u32[]{:S(2)}, u32[]{:S(2)}) collective-permute-start(bf16[4,4,4,64,128]{4,3,2,1,0:T(8,128)(2,1)} %get-tuple-element.28.own_hbm), channel_id=1, source_target_pairs={{8,16},{12,20},{16,8},{20,12},{9,17},{13,21},{17,9},{21,13},{10,18... | collective-permute-start | bytes 3145736 | tf_op jit(solution)/shard_map/ppermute | solution.py:427
  15.5 32.5 %collective-permute-start.7 = (bf16[4,4,4,64,128]{4,3,2,1,0:T(8,128)(2,1)}, bf16[4,4,4,64,128]{4,3,2,1,0:T(8,128)(2,1)}, u32[]{:S(2)}, u32[]{:S(2)}) collective-permute-start(bf16[4,4,4,64,128]{4,3,2,1,0:T(8,128)(2,1)} %get-tuple-element.33), channel_id=1, source_target_pairs={{0,8},{4,12},{8,24},{12,28},{16,0},{20,4},{24,16},{28,20},{1,9},{5... | collective-permute-start | bytes 3145736 | tf_op jit(solution)/shard_map/ppermute | solution.py:427
  21.0 1.2 %copy-start = (bf16[16,256,128]{2,1,0:T(8,128)(2,1)S(1)}, bf16[16,256,128]{2,1,0:T(8,128)(2,1)}, u32[]{:S(2)}) copy-start(bf16[16,256,128]{2,1,0:T(8,128)(2,1)} %rotate_queries.1.query_ref) | copy-start | bytes 3145732
  22.2 12.1 %copy-start.1 = (bf16[16,256,128]{2,1,0:T(8,128)(2,1)S(1)}, bf16[16,256,128]{2,1,0:T(8,128)(2,1)}, u32[]{:S(2)}) copy-start(bf16[16,256,128]{2,1,0:T(8,128)(2,1)} %rotate_queries.1.query_ref) | copy-start | bytes 3145732
  27.6 0.7 %copy-start.6 = (bf16[2,2,256,128]{3,2,1,0:T(8,128)(2,1)}, bf16[2,2,256,128]{3,2,1,0:T(8,128)(2,1)S(1)}, u32[]{:S(2)}) copy-start(bf16[2,2,256,128]{3,2,1,0:T(8,128)(2,1)S(1)} %collective-permute-done.1.rest_1_) | copy-start | bytes 786436
  29.5 0.7 copy-start.4
  30.2 31.9 %collective-permute-start.10 = (bf16[4,4,4,64,128]{4,3,2,1,0:T(8,128)(2,1)}, bf16[4,4,4,64,128]{4,3,2,1,0:T(8,128)(2,1)}, u32[]{:S(2)}, u32[]{:S(2)}) collective-permute-start(bf16[4,4,4,64,128]{4,3,2,1,0:T(8,128)(2,1)} %get-tuple-element.39), channel_id=1, source_target_pairs={{0,12},{4,8},{8,28},{12,24},{16,4},{20,0},{24,20},{28,16},{1,13},{... | collective-permute-start | bytes 3145736 | tf_op jit(solution)/shard_map/ppermute | solution.py:427
  30.2 31.9 %collective-permute-start.9 = (bf16[4,4,4,64,128]{4,3,2,1,0:T(8,128)(2,1)}, bf16[4,4,4,64,128]{4,3,2,1,0:T(8,128)(2,1)}, u32[]{:S(2)}, u32[]{:S(2)}) collective-permute-start(bf16[4,4,4,64,128]{4,3,2,1,0:T(8,128)(2,1)} %get-tuple-element.37), channel_id=1, source_target_pairs={{0,4},{4,0},{8,20},{12,16},{16,12},{20,8},{24,28},{28,24},{1,5},{5... | collective-permute-start | bytes 3145736 | tf_op jit(solution)/shard_map/ppermute | solution.py:427
  31.8 33.5 %collective-permute-start.2 = (bf16[2,2,256,128]{3,2,1,0:T(8,128)(2,1)}, bf16[2,2,256,128]{3,2,1,0:T(8,128)(2,1)}, u32[]{:S(2)}, u32[]{:S(2)}) collective-permute-start(bf16[2,2,256,128]{3,2,1,0:T(8,128)(2,1)} %collective-permute-done.rest_1_), channel_id=1, source_target_pairs={{0,3},{1,2},{2,1},{3,0},{4,7},{5,6},{6,5},{7,4},{8,11},{9,10},{10,... | collective-permute-start | bytes 786440 | tf_op jit(solution)/shard_map/ppermute | solution.py:413
  34.3 1.0 %copy-start.5 = (bf16[2,2,256,128]{3,2,1,0:T(8,128)(2,1)S(1)}, bf16[2,2,256,128]{3,2,1,0:T(8,128)(2,1)}, u32[]{:S(2)}) copy-start(bf16[2,2,256,128]{3,2,1,0:T(8,128)(2,1)} %copy-done.4) | copy-start | bytes 786436
  35.2 0.9 %copy-start.7 = (bf16[2,2,256,128]{3,2,1,0:T(8,128)(2,1)S(1)}, bf16[2,2,256,128]{3,2,1,0:T(8,128)(2,1)}, u32[]{:S(2)}) copy-start(bf16[2,2,256,128]{3,2,1,0:T(8,128)(2,1)} %copy-done.6) | copy-start | bytes 786436
  43.1 0.7 copy-start.8
  43.8 21.5 %collective-permute-start.5 = (bf16[2,2,256,128]{3,2,1,0:T(8,128)(2,1)}, bf16[2,2,256,128]{3,2,1,0:T(8,128)(2,1)}, u32[]{:S(2)}, u32[]{:S(2)}) collective-permute-start(bf16[2,2,256,128]{3,2,1,0:T(8,128)(2,1)} %collective-permute-done.rest_1_), channel_id=1, source_target_pairs={{0,2},{1,3},{2,0},{3,1},{4,6},{5,7},{6,4},{7,5},{8,10},{9,11},{10,... | collective-permute-start | bytes 786440 | tf_op jit(solution)/shard_map/ppermute | solution.py:413
  48.0 17.3 %collective-permute-start.8 = (bf16[2,2,256,128]{3,2,1,0:T(8,128)(2,1)}, bf16[2,2,256,128]{3,2,1,0:T(8,128)(2,1)}, u32[]{:S(2)}, u32[]{:S(2)}) collective-permute-start(bf16[2,2,256,128]{3,2,1,0:T(8,128)(2,1)} %collective-permute-done.rest_1_), channel_id=1, source_target_pairs={{0,1},{1,0},{2,3},{3,2},{4,5},{5,4},{6,7},{7,6},{8,9},{9,8},{10,11... | collective-permute-start | bytes 786440 | tf_op jit(solution)/shard_map/ppermute | solution.py:413
  51.5 13.8 %copy-start.9 = (f32[2,256,128]{2,1,0:T(8,128)S(1)}, f32[2,256,128]{2,1,0:T(8,128)}, u32[]{:S(2)}) copy-start(f32[2,256,128]{2,1,0:T(8,128)} %copy-done.8) | copy-start | bytes 786436

commit v2 on v1

--- a/solution.py
+++ b/solution.py
@@ -433,7 +433,7 @@
     for j in order[:2]:
         hand_over(j, near[-1])
     for j in order[2:3]:
-        hand_over(j, near[-1], own[1], own[hops[1]])
+        hand_over(j, near[-1], own[hops[1]], own[hops[-1]])
     queries = rotate_queries(layer_queries, query_bias, cosine, sine)
     state = attends([((s, 0), near[s]) for s in range(pre_size)], queries=queries, state=None, last=False)
     far = []
@@ -442,16 +442,19 @@
             wait = (own[r], state[0]) if r == hops[1] else (own[r], arrived[order[0]])
             far.append(((s, r), swap(after(near[s], *wait), "rep", rep_size, r)))
     for j in order[3:]:
-        hand_over(j, near[-1], state[0], own[hops[-1]])
-    state = attends([((0, r), own[r]) for r in hops], queries=queries, state=state, last=False)
+        hand_over(j, near[-1], state[0], own[1])
     for s in range(1, pre_size):
-        far.append(((s, 1), swap(after(near[s], state[0], arrived[order[1]]), "rep", rep_size, 1)))
+        far.append(((s, 1), swap(after(near[s], own[1], arrived[order[1]]), "rep", rep_size, 1)))
+    ready = (after(state[0], arrived[order[0]], arrived[order[1]]), state[1])
+    state = attends([((0, r), own[r]) for r in hops], queries=queries, state=ready, last=False)
     state = attends(far, queries=queries, state=state, last=True)
     split = dec_size // 2
     arrange = functools.partial(place, (blk_count, capacity, hl, group), pre_size)
     got = [arrived[j] for j in order]
     decode_cache = arrange(order[:split], order, page_table, sends[0], got[:split], None)
-    decode_cache = arrange(order[split:], [], page_table, sends[0], got[split:], decode_cache)
+    decode_cache = arrange(
+        order[split:], [], page_table, sends[0], got[split:], after(decode_cache, state)
+    )
     return (state, decode_cache)
 
 

time: 74.5 us -> 73.5 us (0.987)
  waiting for transfers between devices: 12.8 us -> 11.5 us
  local copies, waits for them, and re-layouts: 5.32 us -> 6.19 us
    ppermute x4, waiting for transfers between devices: 10.7 us -> 4.89 us  [hand_over(): arrived[j] = lax.ppermute(after(sends[j], *before), ('pre', 'dec'), route)]
    ppermute x7, waiting for transfers between devices: 2.11 us -> 6.65 us  [shards(): lax.ppermute(value, axis, [(i, i ^ hop) for i in range(size)])]
    ppermute x7, starting transfers between devices: 14.3 us -> 13.3 us  [shards(): lax.ppermute(value, axis, [(i, i ^ hop) for i in range(size)])]
    unnamed x22, local copies, waits for them, and re-layouts: 5.32 us -> 6.19 us
  transfers between devices with their start and end apart: 11 -> 11, of which waited for: 3 -> 3; matrix products, arithmetic and copies ran while one was open for 0% -> 0% of each run, Pallas kernels for 32% -> 40%
where the time goes in v2:
time: 73.5 us; the launch traced here: 72.8 us
  Pallas kernels  34.8 us (47%)
  starting transfers between devices  19.6 us (27%)
  waiting for transfers between devices  11.5 us (16%)
  local copies, waits for them, and re-layouts  6.19 us (8%)
  between operations  0.76 us (1%)
    pallas_call x3, Pallas kernels, attend(): pl.pallas_call(functools.partial(attend_kernel, moves, rep_size, first, l...  19.8 us
    ppermute x7, starting transfers between devices, shards(): lax.ppermute(value, axis, [(i, i ^ hop) for i in range(size)])  13.3 us
    ppermute x7, waiting for transfers between devices, shards(): lax.ppermute(value, axis, [(i, i ^ hop) for i in range(size)])  6.65 us
    pallas_call x2, Pallas kernels, place(): pl.pallas_call(functools.partial(place_kernel, dims, here, rest_j), out_s...  6.37 us
    ppermute x4, starting transfers between devices, hand_over(): arrived[j] = lax.ppermute(after(sends[j], *before), ('pre', 'dec'), route)  6.26 us
    unnamed x22, local copies, waits for them, and re-layouts  6.19 us
    ppermute x4, waiting for transfers between devices, hand_over(): arrived[j] = lax.ppermute(after(sends[j], *before), ('pre', 'dec'), route)  4.89 us
    pallas_call x1, Pallas kernels, pack(): pl.pallas_call(functools.partial(pack_kernel, dims), out_shape=[jax.Shape...  3.17 us
  transfers between devices with their start and end apart: 11, of which 3 were waited for; matrix products, arithmetic and copies ran while one was open for 0% of the time, Pallas kernels for 40%

profile of v2, /device:TPU:0, one launch (start us, length us, event | category | flops | bytes accessed | tf_op | source)
XLA Modules:
  0.0 72.8 jit_solution(15896307400772688280)
XLA Ops:
  0.6 2.6 %turn.1 = (bf16[2,2,256,128]{3,2,1,0:T(8,128)(2,1)}, f32[256,128]{1,0:T(8,128)}, f32[256,128]{1,0:T(8,128)}, s32[256,128]{1,0:T(8,128)}) custom-call(s32[16,128]{1,0:T(8,128)} %bitcast.4, f32[1,128]{1,0:T(1,128)} %constant.2.clone.freq_ref, f32[1,1024]{1,0:T(1,128)} %bitcast.9, f32[1,1024]{1,0:T(1,128)} %bitcast.10, bf16[256,1024]{1,0:T(8,128)(2,1)} %keys_hbm.1, ...), custom_call_target="tpu_custom_call" | custom-call | flops 1 | bytes 1 | tf_op jit(solution)/shard_map/turn/pallas_call | solution.py:86
  3.2 0.0 copy-start.10
  3.3 3.0 %collective-permute-start = (bf16[2,2,256,128]{3,2,1,0:T(8,128)(2,1)}, bf16[2,2,256,128]{3,2,1,0:T(8,128)(2,1)}, u32[]{:S(2)}, u32[]{:S(2)}) collective-permute-start(bf16[2,2,256,128]{3,2,1,0:T(8,128)(2,1)} %get-tuple-element.26.rest_0_.kv_hbm), channel_id=1, source_target_pairs={{0,16},{16,0},{1,17},{17,1},{2,18},{18,2},{3,19},{19,3},{4,20},{20... | collective-permute-start | bytes 786440 | tf_op jit(solution)/shard_map/ppermute | solution.py:413
  6.3 2.6 %collective-permute-start.3 = (bf16[2,2,256,128]{3,2,1,0:T(8,128)(2,1)}, bf16[2,2,256,128]{3,2,1,0:T(8,128)(2,1)S(1)}, u32[]{:S(2)}, u32[]{:S(2)}) collective-permute-start(bf16[2,2,256,128]{3,2,1,0:T(8,128)(2,1)} %get-tuple-element.26.rest_0_.kv_hbm), channel_id=1, source_target_pairs={{0,2},{1,3},{2,0},{3,1},{4,6},{5,7},{6,4},{7,5},{8,10},{9,11},{10,... | collective-permute-start | bytes 786440 | tf_op jit(solution)/shard_map/ppermute | solution.py:413
  8.9 1.3 %collective-permute-start.1 = (bf16[2,2,256,128]{3,2,1,0:T(8,128)(2,1)}, bf16[2,2,256,128]{3,2,1,0:T(8,128)(2,1)S(1)}, u32[]{:S(2)}, u32[]{:S(2)}) collective-permute-start(bf16[2,2,256,128]{3,2,1,0:T(8,128)(2,1)} %get-tuple-element.26.rest_0_.kv_hbm), channel_id=1, source_target_pairs={{0,3},{1,2},{2,1},{3,0},{4,7},{5,6},{6,5},{7,4},{8,11},{9,10},{10,... | collective-permute-start | bytes 786440 | tf_op jit(solution)/shard_map/ppermute | solution.py:413
  10.2 3.2 %pack.1 = (bf16[4,4,4,64,128]{4,3,2,1,0:T(8,128)(2,1)}, bf16[4,4,4,64,128]{4,3,2,1,0:T(8,128)(2,1)}, bf16[4,4,4,64,128]{4,3,2,1,0:T(8,128)(2,1)}, bf16[4,4,4,64,128]{4,3,2,1,0:T(8,128)(2,1)}) custom-call(s32[4,16]{1,0:T(4,128)} %page_ref.5, s32[32]{0:T(128)} %lengths_ref.1, s32[32]{0:T(128)} %replica_ref.1, ...), custom_call_target="tpu_custom_call" | custom-call | flops 1 | bytes 1 | tf_op jit(solution)/shard_map/pack/pallas_call | solution.py:170
  13.4 0.0 collective-permute-done.rest_1_
  13.4 1.7 %collective-permute-start.4 = (bf16[4,4,4,64,128]{4,3,2,1,0:T(8,128)(2,1)}, bf16[4,4,4,64,128]{4,3,2,1,0:T(8,128)(2,1)}, u32[]{:S(2)}, u32[]{:S(2)}) collective-permute-start(bf16[4,4,4,64,128]{4,3,2,1,0:T(8,128)(2,1)} %get-tuple-element.30.own_hbm), channel_id=1, source_target_pairs={{8,16},{12,20},{16,8},{20,12},{9,17},{13,21},{17,9},{21,13},{10,18... | collective-permute-start | bytes 3145736 | tf_op jit(solution)/shard_map/ppermute | solution.py:427
  15.1 3.0 %collective-permute-start.7 = (bf16[4,4,4,64,128]{4,3,2,1,0:T(8,128)(2,1)}, bf16[4,4,4,64,128]{4,3,2,1,0:T(8,128)(2,1)}, u32[]{:S(2)}, u32[]{:S(2)}) collective-permute-start(bf16[4,4,4,64,128]{4,3,2,1,0:T(8,128)(2,1)} %get-tuple-element.33), channel_id=1, source_target_pairs={{0,8},{4,12},{8,24},{12,28},{16,0},{20,4},{24,16},{28,20},{1,9},{5... | collective-permute-start | bytes 3145736 | tf_op jit(solution)/shard_map/ppermute | solution.py:427
  18.1 1.6 %collective-permute-start.6 = (bf16[2,2,256,128]{3,2,1,0:T(8,128)(2,1)S(1)}, bf16[2,2,256,128]{3,2,1,0:T(8,128)(2,1)S(1)}, u32[]{:S(2)}, u32[]{:S(2)}) collective-permute-start(bf16[2,2,256,128]{3,2,1,0:T(8,128)(2,1)S(1)} %copy-done.3), channel_id=1, source_target_pairs={{0,1},{1,0},{2,3},{3,2},{4,5},{5,4},{6,7},{7,6},{8,9},{9,8},{10,11... | collective-permute-start | bytes 786440 | tf_op jit(solution)/shard_map/ppermute | solution.py:413
  19.6 2.9 %rotate_queries.1.query_ref = bf16[16,256,128]{2,1,0:T(8,128)(2,1)} custom-call(bf16[256,2048]{1,0:T(8,128)(2,1)} %query_ref.1, f32[1,2048]{1,0:T(1,128)} %bitcast.8, f32[256,128]{1,0:T(8,128)} %get-tuple-element.23.cos_ref, f32[256,128]{1,0:T(8,128)} %get-tuple-element.24.sin_ref), custom_call_target="tpu_custom_call" | custom-call | flops 1 | bytes 1 | tf_op jit(solution)/shard_map/rotate_queries/pallas_call | solution.py:200
  22.5 1.2 %copy-done = bf16[16,256,128]{2,1,0:T(8,128)(2,1)S(1)} copy-done((bf16[16,256,128]{2,1,0:T(8,128)(2,1)S(1)}, bf16[16,256,128]{2,1,0:T(8,128)(2,1)}, u32[]{:S(2)}) %copy-start) | copy-done | bytes 1048600
  23.7 4.3 %attend.3 = (f32[2,256,128]{2,1,0:T(8,128)S(1)}, f32[16,256,128]{2,1,0:T(8,128)S(1)}) custom-call(bf16[16,256,128]{2,1,0:T(8,128)(2,1)S(1)} %copy-done, s32[256,128]{1,0:T(8,128)S(1)} %copy-done.2, s32[16,128]{1,0:T(8,128)S(1)} %bitcast.5, bf16[2,2,256,128]{3,2,1,0:T(8,128)(2,1)S(1)} %copy-done.3, bf16[2,2,256,128]{3,2,1,0:T(8,128)(2,1)} %collective-permute-done.rest_1_), custom_call_target="tpu_custom_call" | custom-call | flops 1 | bytes 1 | tf_op jit(solution)/shard_map/attend/pallas_call | solution.py:285
  28.1 0.7 copy-done.8
  28.8 0.7 copy-done.4
  29.5 2.5 %collective-permute-done.6.rest_0_ = bf16[2,2,256,128]{3,2,1,0:T(8,128)(2,1)S(1)} collective-permute-done((bf16[2,2,256,128]{3,2,1,0:T(8,128)(2,1)S(1)}, bf16[2,2,256,128]{3,2,1,0:T(8,128)(2,1)S(1)}, u32[]{:S(2)}, u32[]{:S(2)}) %collective-permute-start.6) | collective-permute-done | bytes 262176 | tf_op jit(solution)/shard_map/ppermute | solution.py:413
  32.0 0.7 copy-done.6
  32.8 1.2 %collective-permute-start.10 = (bf16[4,4,4,64,128]{4,3,2,1,0:T(8,128)(2,1)}, bf16[4,4,4,64,128]{4,3,2,1,0:T(8,128)(2,1)}, u32[]{:S(2)}, u32[]{:S(2)}) collective-permute-start(bf16[4,4,4,64,128]{4,3,2,1,0:T(8,128)(2,1)} %get-tuple-element.42), channel_id=1, source_target_pairs={{0,12},{4,8},{8,28},{12,24},{16,4},{20,0},{24,20},{28,16},{1,13},{... | collective-permute-start | bytes 3145736 | tf_op jit(solution)/shard_map/ppermute | solution.py:427
  34.0 0.4 collective-permute-start.9
  34.4 3.5 %collective-permute-start.2 = (bf16[2,2,256,128]{3,2,1,0:T(8,128)(2,1)}, bf16[2,2,256,128]{3,2,1,0:T(8,128)(2,1)}, u32[]{:S(2)}, u32[]{:S(2)}) collective-permute-start(bf16[2,2,256,128]{3,2,1,0:T(8,128)(2,1)} %collective-permute-done.rest_1_), channel_id=1, source_target_pairs={{0,3},{1,2},{2,1},{3,0},{4,7},{5,6},{6,5},{7,4},{8,11},{9,10},{10,... | collective-permute-start | bytes 786440 | tf_op jit(solution)/shard_map/ppermute | solution.py:413
  37.8 4.9 %collective-permute-done.7.rest_1_ = bf16[4,4,4,64,128]{4,3,2,1,0:T(8,128)(2,1)} collective-permute-done((bf16[4,4,4,64,128]{4,3,2,1,0:T(8,128)(2,1)}, bf16[4,4,4,64,128]{4,3,2,1,0:T(8,128)(2,1)}, u32[]{:S(2)}, u32[]{:S(2)}) %collective-permute-start.7) | collective-permute-done | bytes 1048608 | tf_op jit(solution)/shard_map/ppermute | solution.py:427
  42.7 1.3 %collective-permute-start.8 = (bf16[2,2,256,128]{3,2,1,0:T(8,128)(2,1)}, bf16[2,2,256,128]{3,2,1,0:T(8,128)(2,1)}, u32[]{:S(2)}, u32[]{:S(2)}) collective-permute-start(bf16[2,2,256,128]{3,2,1,0:T(8,128)(2,1)} %collective-permute-done.rest_1_), channel_id=1, source_target_pairs={{0,1},{1,0},{2,3},{3,2},{4,5},{5,4},{6,7},{7,6},{8,9},{9,8},{10,11... | collective-permute-start | bytes 786440 | tf_op jit(solution)/shard_map/ppermute | solution.py:413
  44.0 3.6 %place.2.rest_2_ = bf16[1,1,8,8,4,64,128]{6,5,4,3,2,1,0:T(8,128)(2,1)} custom-call(s32[4,16]{1,0:T(4,128)} %page_ref.5, bf16[4,4,4,64,128]{4,3,2,1,0:T(8,128)(2,1)} %get-tuple-element.30.own_hbm, bf16[4,4,4,64,128]{4,3,2,1,0:T(8,128)(2,1)} %collective-permute-done.4.rest_0_, bf16[4,4,4,64,128]{4,3,2,1,0:T(8,128)(2,1)} %collective-permute-done.7.rest_1_), custom_call_target="tpu_custom_call" | custom-call | flops 1 | bytes 1 | tf_op jit(solution)/shard_map/place/pallas_call | solution.py:369
  47.6 0.9 %copy-done.5 = bf16[2,2,256,128]{3,2,1,0:T(8,128)(2,1)S(1)} copy-done((bf16[2,2,256,128]{3,2,1,0:T(8,128)(2,1)S(1)}, bf16[2,2,256,128]{3,2,1,0:T(8,128)(2,1)}, u32[]{:S(2)}) %copy-start.5) | copy-done | bytes 262168
  48.6 0.9 %copy-done.7 = bf16[2,2,256,128]{3,2,1,0:T(8,128)(2,1)S(1)} copy-done((bf16[2,2,256,128]{3,2,1,0:T(8,128)(2,1)S(1)}, bf16[2,2,256,128]{3,2,1,0:T(8,128)(2,1)}, u32[]{:S(2)}) %copy-start.7) | copy-done | bytes 262168
  49.5 0.9 %copy-done.9 = f32[2,256,128]{2,1,0:T(8,128)S(1)} copy-done((f32[2,256,128]{2,1,0:T(8,128)S(1)}, f32[2,256,128]{2,1,0:T(8,128)}, u32[]{:S(2)}) %copy-start.9) | copy-done | bytes 262168
  50.5 6.9 %attend.4 = (f32[2,256,128]{2,1,0:T(8,128)S(1)}, f32[16,256,128]{2,1,0:T(8,128)S(1)}) custom-call(bf16[16,256,128]{2,1,0:T(8,128)(2,1)S(1)} %copy-done.1, s32[256,128]{1,0:T(8,128)S(1)} %copy-done.2, s32[16,128]{1,0:T(8,128)S(1)} %bitcast.6, bf16[2,2,256,128]{3,2,1,0:T(8,128)(2,1)S(1)} %copy-done.7, bf16[2,2,256,128]{3,2,1,0:T(8,128)(2,1)S(1)} %copy-done.5, ...), custom_call_target="tpu_custom_call" | custom-call | flops 1 | bytes 1 | tf_op jit(solution)/shard_map/attend/pallas_call | solution.py:285
  57.3 0.0 collective-permute-done.2.rest_0_
  57.4 4.1 %collective-permute-done.5.rest_1_ = bf16[2,2,256,128]{3,2,1,0:T(8,128)(2,1)} collective-permute-done((bf16[2,2,256,128]{3,2,1,0:T(8,128)(2,1)}, bf16[2,2,256,128]{3,2,1,0:T(8,128)(2,1)}, u32[]{:S(2)}, u32[]{:S(2)}) %collective-permute-start.5) | collective-permute-done | bytes 262176 | tf_op jit(solution)/shard_map/ppermute | solution.py:413
  61.4 0.0 collective-permute-done.8.rest_2_
  61.4 8.6 %attend.5 = bf16[256,2048]{1,0:T(8,128)(2,1)} custom-call(bf16[16,256,128]{2,1,0:T(8,128)(2,1)S(1)} %copy-done.1, s32[256,128]{1,0:T(8,128)S(1)} %copy-done.2, s32[16,128]{1,0:T(8,128)S(1)} %bitcast.7, bf16[2,2,256,128]{3,2,1,0:T(8,128)(2,1)} %collective-permute-done.2.rest_0_, bf16[2,2,256,128]{3,2,1,0:T(8,128)(2,1)} %collective-permute-done.5.rest_1_, ...), custom_call_target="tpu_custom_call" | custom-call | flops 1 | bytes 1 | tf_op jit(solution)/shard_map/attend/pallas_call | solution.py:285
  70.0 2.8 %place.3 = bf16[1,1,8,8,4,64,128]{6,5,4,3,2,1,0:T(8,128)(2,1)} custom-call(s32[4,16]{1,0:T(4,128)} %page_ref.5, bf16[4,4,4,64,128]{4,3,2,1,0:T(8,128)(2,1)} %get-tuple-element.30.own_hbm, bf16[4,4,4,64,128]{4,3,2,1,0:T(8,128)(2,1)} %collective-permute-done.9.rest_0_, ...), custom_call_target="tpu_custom_call", output_to_operand_aliasing={{}: (4, {})} | custom-call | flops 1 | bytes 1 | tf_op jit(solution)/shard_map/place/pallas_call | solution.py:369
  (20 shorter events, 0.0 us)
Async XLA Ops:
  3.2 14.8 %copy-start.3 = (bf16[2,2,256,128]{3,2,1,0:T(8,128)(2,1)S(1)}, bf16[2,2,256,128]{3,2,1,0:T(8,128)(2,1)}, u32[]{:S(2)}) copy-start(bf16[2,2,256,128]{3,2,1,0:T(8,128)(2,1)} %get-tuple-element.26.rest_0_.kv_hbm) | copy-start | bytes 786436
  3.2 19.3 %copy-start.2 = (s32[256,128]{1,0:T(8,128)S(1)}, s32[256,128]{1,0:T(8,128)}, u32[]{:S(2)}) copy-start(s32[256,128]{1,0:T(8,128)} %get-tuple-element.25.qpos_ref) | copy-start | bytes 393220
  3.2 19.3 %copy-start.10 = (s32[2048]{0:T(1024)S(1)}, s32[2048]{0:T(1024)}, u32[]{:S(2)}) copy-start(s32[2048]{0:T(1024)} %param.18) | copy-start | bytes 24580
  3.3 10.1 %collective-permute-start = (bf16[2,2,256,128]{3,2,1,0:T(8,128)(2,1)}, bf16[2,2,256,128]{3,2,1,0:T(8,128)(2,1)}, u32[]{:S(2)}, u32[]{:S(2)}) collective-permute-start(bf16[2,2,256,128]{3,2,1,0:T(8,128)(2,1)} %get-tuple-element.26.rest_0_.kv_hbm), channel_id=1, source_target_pairs={{0,16},{16,0},{1,17},{17,1},{2,18},{18,2},{3,19},{19,3},{4,20},{20... | collective-permute-start | bytes 786440 | tf_op jit(solution)/shard_map/ppermute | solution.py:413
  6.3 22.5 %collective-permute-start.3 = (bf16[2,2,256,128]{3,2,1,0:T(8,128)(2,1)}, bf16[2,2,256,128]{3,2,1,0:T(8,128)(2,1)S(1)}, u32[]{:S(2)}, u32[]{:S(2)}) collective-permute-start(bf16[2,2,256,128]{3,2,1,0:T(8,128)(2,1)} %get-tuple-element.26.rest_0_.kv_hbm), channel_id=1, source_target_pairs={{0,2},{1,3},{2,0},{3,1},{4,6},{5,7},{6,4},{7,5},{8,10},{9,11},{10,... | collective-permute-start | bytes 786440 | tf_op jit(solution)/shard_map/ppermute | solution.py:413
  8.9 19.9 %collective-permute-start.1 = (bf16[2,2,256,128]{3,2,1,0:T(8,128)(2,1)}, bf16[2,2,256,128]{3,2,1,0:T(8,128)(2,1)S(1)}, u32[]{:S(2)}, u32[]{:S(2)}) collective-permute-start(bf16[2,2,256,128]{3,2,1,0:T(8,128)(2,1)} %get-tuple-element.26.rest_0_.kv_hbm), channel_id=1, source_target_pairs={{0,3},{1,2},{2,1},{3,0},{4,7},{5,6},{6,5},{7,4},{8,11},{9,10},{10,... | collective-permute-start | bytes 786440 | tf_op jit(solution)/shard_map/ppermute | solution.py:413
  13.4 24.4 %collective-permute-start.4 = (bf16[4,4,4,64,128]{4,3,2,1,0:T(8,128)(2,1)}, bf16[4,4,4,64,128]{4,3,2,1,0:T(8,128)(2,1)}, u32[]{:S(2)}, u32[]{:S(2)}) collective-permute-start(bf16[4,4,4,64,128]{4,3,2,1,0:T(8,128)(2,1)} %get-tuple-element.30.own_hbm), channel_id=1, source_target_pairs={{8,16},{12,20},{16,8},{20,12},{9,17},{13,21},{17,9},{21,13},{10,18... | collective-permute-start | bytes 3145736 | tf_op jit(solution)/shard_map/ppermute | solution.py:427
  15.1 27.7 %collective-permute-start.7 = (bf16[4,4,4,64,128]{4,3,2,1,0:T(8,128)(2,1)}, bf16[4,4,4,64,128]{4,3,2,1,0:T(8,128)(2,1)}, u32[]{:S(2)}, u32[]{:S(2)}) collective-permute-start(bf16[4,4,4,64,128]{4,3,2,1,0:T(8,128)(2,1)} %get-tuple-element.33), channel_id=1, source_target_pairs={{0,8},{4,12},{8,24},{12,28},{16,0},{20,4},{24,16},{28,20},{1,9},{5... | collective-permute-start | bytes 3145736 | tf_op jit(solution)/shard_map/ppermute | solution.py:427
  18.1 14.0 %collective-permute-start.6 = (bf16[2,2,256,128]{3,2,1,0:T(8,128)(2,1)S(1)}, bf16[2,2,256,128]{3,2,1,0:T(8,128)(2,1)S(1)}, u32[]{:S(2)}, u32[]{:S(2)}) collective-permute-start(bf16[2,2,256,128]{3,2,1,0:T(8,128)(2,1)S(1)} %copy-done.3), channel_id=1, source_target_pairs={{0,1},{1,0},{2,3},{3,2},{4,5},{5,4},{6,7},{7,6},{8,9},{9,8},{10,11... | collective-permute-start | bytes 786440 | tf_op jit(solution)/shard_map/ppermute | solution.py:413
  22.5 1.2 %copy-start = (bf16[16,256,128]{2,1,0:T(8,128)(2,1)S(1)}, bf16[16,256,128]{2,1,0:T(8,128)(2,1)}, u32[]{:S(2)}) copy-start(bf16[16,256,128]{2,1,0:T(8,128)(2,1)} %rotate_queries.1.query_ref) | copy-start | bytes 3145732
  28.1 0.7 copy-start.8
  28.8 0.7 copy-start.4
  32.0 0.7 copy-start.6
  32.8 14.9 %copy-start.1 = (bf16[16,256,128]{2,1,0:T(8,128)(2,1)S(1)}, bf16[16,256,128]{2,1,0:T(8,128)(2,1)}, u32[]{:S(2)}) copy-start(bf16[16,256,128]{2,1,0:T(8,128)(2,1)} %rotate_queries.1.query_ref) | copy-start | bytes 3145732
  32.8 37.3 %collective-permute-start.10 = (bf16[4,4,4,64,128]{4,3,2,1,0:T(8,128)(2,1)}, bf16[4,4,4,64,128]{4,3,2,1,0:T(8,128)(2,1)}, u32[]{:S(2)}, u32[]{:S(2)}) collective-permute-start(bf16[4,4,4,64,128]{4,3,2,1,0:T(8,128)(2,1)} %get-tuple-element.42), channel_id=1, source_target_pairs={{0,12},{4,8},{8,28},{12,24},{16,4},{20,0},{24,20},{28,16},{1,13},{... | collective-permute-start | bytes 3145736 | tf_op jit(solution)/shard_map/ppermute | solution.py:427
  34.0 36.1 %collective-permute-start.9 = (bf16[4,4,4,64,128]{4,3,2,1,0:T(8,128)(2,1)}, bf16[4,4,4,64,128]{4,3,2,1,0:T(8,128)(2,1)}, u32[]{:S(2)}, u32[]{:S(2)}) collective-permute-start(bf16[4,4,4,64,128]{4,3,2,1,0:T(8,128)(2,1)} %get-tuple-element.40), channel_id=1, source_target_pairs={{0,4},{4,0},{8,20},{12,16},{16,12},{20,8},{24,28},{28,24},{1,5},{5... | collective-permute-start | bytes 3145736 | tf_op jit(solution)/shard_map/ppermute | solution.py:427
  34.4 23.0 %collective-permute-start.2 = (bf16[2,2,256,128]{3,2,1,0:T(8,128)(2,1)}, bf16[2,2,256,128]{3,2,1,0:T(8,128)(2,1)}, u32[]{:S(2)}, u32[]{:S(2)}) collective-permute-start(bf16[2,2,256,128]{3,2,1,0:T(8,128)(2,1)} %collective-permute-done.rest_1_), channel_id=1, source_target_pairs={{0,3},{1,2},{2,1},{3,0},{4,7},{5,6},{6,5},{7,4},{8,11},{9,10},{10,... | collective-permute-start | bytes 786440 | tf_op jit(solution)/shard_map/ppermute | solution.py:413
  37.8 23.6 %collective-permute-start.5 = (bf16[2,2,256,128]{3,2,1,0:T(8,128)(2,1)}, bf16[2,2,256,128]{3,2,1,0:T(8,128)(2,1)}, u32[]{:S(2)}, u32[]{:S(2)}) collective-permute-start(bf16[2,2,256,128]{3,2,1,0:T(8,128)(2,1)} %collective-permute-done.rest_1_), channel_id=1, source_target_pairs={{0,2},{1,3},{2,0},{3,1},{4,6},{5,7},{6,4},{7,5},{8,10},{9,11},{10,... | collective-permute-start | bytes 786440 | tf_op jit(solution)/shard_map/ppermute | solution.py:413
  42.7 18.7 %collective-permute-start.8 = (bf16[2,2,256,128]{3,2,1,0:T(8,128)(2,1)}, bf16[2,2,256,128]{3,2,1,0:T(8,128)(2,1)}, u32[]{:S(2)}, u32[]{:S(2)}) collective-permute-start(bf16[2,2,256,128]{3,2,1,0:T(8,128)(2,1)} %collective-permute-done.rest_1_), channel_id=1, source_target_pairs={{0,1},{1,0},{2,3},{3,2},{4,5},{5,4},{6,7},{7,6},{8,9},{9,8},{10,11... | collective-permute-start | bytes 786440 | tf_op jit(solution)/shard_map/ppermute | solution.py:413
  47.6 1.0 %copy-start.5 = (bf16[2,2,256,128]{3,2,1,0:T(8,128)(2,1)S(1)}, bf16[2,2,256,128]{3,2,1,0:T(8,128)(2,1)}, u32[]{:S(2)}) copy-start(bf16[2,2,256,128]{3,2,1,0:T(8,128)(2,1)} %copy-done.4) | copy-start | bytes 786436
  48.6 0.9 %copy-start.7 = (bf16[2,2,256,128]{3,2,1,0:T(8,128)(2,1)S(1)}, bf16[2,2,256,128]{3,2,1,0:T(8,128)(2,1)}, u32[]{:S(2)}) copy-start(bf16[2,2,256,128]{3,2,1,0:T(8,128)(2,1)} %copy-done.6) | copy-start | bytes 786436
  49.5 0.9 %copy-start.9 = (f32[2,256,128]{2,1,0:T(8,128)S(1)}, f32[2,256,128]{2,1,0:T(8,128)}, u32[]{:S(2)}) copy-start(f32[2,256,128]{2,1,0:T(8,128)} %copy-done.8) | copy-start | bytes 786436

commit v3 on v2

--- a/solution.py
+++ b/solution.py
@@ -433,7 +433,7 @@
     for j in order[:2]:
         hand_over(j, near[-1])
     for j in order[2:3]:
-        hand_over(j, near[-1], own[hops[1]], own[hops[-1]])
+        hand_over(j, near[-1], own[hops[1]], own[hops[-1]], own[1])
     queries = rotate_queries(layer_queries, query_bias, cosine, sine)
     state = attends([((s, 0), near[s]) for s in range(pre_size)], queries=queries, state=None, last=False)
     far = []
@@ -442,7 +442,7 @@
             wait = (own[r], state[0]) if r == hops[1] else (own[r], arrived[order[0]])
             far.append(((s, r), swap(after(near[s], *wait), "rep", rep_size, r)))
     for j in order[3:]:
-        hand_over(j, near[-1], state[0], own[1])
+        hand_over(j, near[-1], state[0], own[1], own[hops[-1]])
     for s in range(1, pre_size):
         far.append(((s, 1), swap(after(near[s], own[1], arrived[order[1]]), "rep", rep_size, 1)))
     ready = (after(state[0], arrived[order[0]], arrived[order[1]]), state[1])

time: 73.5 us -> 71.9 us (0.978)
  waiting for transfers between devices: 11.5 us -> 9.93 us
    ppermute x7, waiting for transfers between devices: 6.65 us -> 4.47 us  [shards(): lax.ppermute(value, axis, [(i, i ^ hop) for i in range(size)])]
  transfers between devices with their start and end apart: 11 -> 11, of which waited for: 3 -> 3; matrix products, arithmetic and copies ran while one was open for 0% -> 0% of each run, Pallas kernels for 40% -> 42%
where the time goes in v3:
time: 71.9 us; the launch traced here: 71.1 us
  Pallas kernels  35 us (49%)
  starting transfers between devices  19.3 us (27%)
  waiting for transfers between devices  9.93 us (14%)
  local copies, waits for them, and re-layouts  6.21 us (9%)
  between operations  0.77 us (1%)
    pallas_call x3, Pallas kernels, attend(): pl.pallas_call(functools.partial(attend_kernel, moves, rep_size, first, l...  20 us
    ppermute x7, starting transfers between devices, shards(): lax.ppermute(value, axis, [(i, i ^ hop) for i in range(size)])  13.5 us
    pallas_call x2, Pallas kernels, place(): pl.pallas_call(functools.partial(place_kernel, dims, here, rest_j), out_s...  6.37 us
    unnamed x22, local copies, waits for them, and re-layouts  6.21 us
    ppermute x4, starting transfers between devices, hand_over(): arrived[j] = lax.ppermute(after(sends[j], *before), ('pre', 'dec'), route)  5.82 us
    ppermute x4, waiting for transfers between devices, hand_over(): arrived[j] = lax.ppermute(after(sends[j], *before), ('pre', 'dec'), route)  5.46 us
    ppermute x7, waiting for transfers between devices, shards(): lax.ppermute(value, axis, [(i, i ^ hop) for i in range(size)])  4.47 us
    pallas_call x1, Pallas kernels, pack(): pl.pallas_call(functools.partial(pack_kernel, dims), out_shape=[jax.Shape...  3.16 us
  transfers between devices with their start and end apart: 11, of which 3 were waited for; matrix products, arithmetic and copies ran while one was open for 0% of the time, Pallas kernels for 42%

profile of v3, /device:TPU:0, one launch (start us, length us, event | category | flops | bytes accessed | tf_op | source)
XLA Modules:
  0.0 71.1 jit_solution(3127261468764386184)
XLA Ops:
  0.6 2.6 %turn.1 = (bf16[2,2,256,128]{3,2,1,0:T(8,128)(2,1)}, f32[256,128]{1,0:T(8,128)}, f32[256,128]{1,0:T(8,128)}, s32[256,128]{1,0:T(8,128)}) custom-call(s32[16,128]{1,0:T(8,128)} %bitcast.4, f32[1,128]{1,0:T(1,128)} %constant.2.clone.freq_ref, f32[1,1024]{1,0:T(1,128)} %bitcast.9, f32[1,1024]{1,0:T(1,128)} %bitcast.10, bf16[256,1024]{1,0:T(8,128)(2,1)} %keys_hbm.1, ...), custom_call_target="tpu_custom_call" | custom-call | flops 1 | bytes 1 | tf_op jit(solution)/shard_map/turn/pallas_call | solution.py:86
  3.2 0.0 copy-start.10
  3.3 3.0 %collective-permute-start = (bf16[2,2,256,128]{3,2,1,0:T(8,128)(2,1)}, bf16[2,2,256,128]{3,2,1,0:T(8,128)(2,1)}, u32[]{:S(2)}, u32[]{:S(2)}) collective-permute-start(bf16[2,2,256,128]{3,2,1,0:T(8,128)(2,1)} %get-tuple-element.26.rest_0_.kv_hbm), channel_id=1, source_target_pairs={{0,16},{16,0},{1,17},{17,1},{2,18},{18,2},{3,19},{19,3},{4,20},{20... | collective-permute-start | bytes 786440 | tf_op jit(solution)/shard_map/ppermute | solution.py:413
  6.3 1.6 %collective-permute-start.6 = (bf16[2,2,256,128]{3,2,1,0:T(8,128)(2,1)}, bf16[2,2,256,128]{3,2,1,0:T(8,128)(2,1)S(1)}, u32[]{:S(2)}, u32[]{:S(2)}) collective-permute-start(bf16[2,2,256,128]{3,2,1,0:T(8,128)(2,1)} %get-tuple-element.26.rest_0_.kv_hbm), channel_id=1, source_target_pairs={{0,1},{1,0},{2,3},{3,2},{4,5},{5,4},{6,7},{7,6},{8,9},{9,8},{10,11... | collective-permute-start | bytes 786440 | tf_op jit(solution)/shard_map/ppermute | solution.py:413
  7.9 2.6 %collective-permute-start.3 = (bf16[2,2,256,128]{3,2,1,0:T(8,128)(2,1)}, bf16[2,2,256,128]{3,2,1,0:T(8,128)(2,1)S(1)}, u32[]{:S(2)}, u32[]{:S(2)}) collective-permute-start(bf16[2,2,256,128]{3,2,1,0:T(8,128)(2,1)} %get-tuple-element.26.rest_0_.kv_hbm), channel_id=1, source_target_pairs={{0,2},{1,3},{2,0},{3,1},{4,6},{5,7},{6,4},{7,5},{8,10},{9,11},{10,... | collective-permute-start | bytes 786440 | tf_op jit(solution)/shard_map/ppermute | solution.py:413
  10.5 0.2 collective-permute-start.1
  10.7 3.2 %pack.1 = (bf16[4,4,4,64,128]{4,3,2,1,0:T(8,128)(2,1)}, bf16[4,4,4,64,128]{4,3,2,1,0:T(8,128)(2,1)}, bf16[4,4,4,64,128]{4,3,2,1,0:T(8,128)(2,1)}, bf16[4,4,4,64,128]{4,3,2,1,0:T(8,128)(2,1)}) custom-call(s32[4,16]{1,0:T(4,128)} %page_ref.5, s32[32]{0:T(128)} %lengths_ref.1, s32[32]{0:T(128)} %replica_ref.1, ...), custom_call_target="tpu_custom_call" | custom-call | flops 1 | bytes 1 | tf_op jit(solution)/shard_map/pack/pallas_call | solution.py:170
  13.8 0.0 collective-permute-done.rest_1_
  13.9 1.7 %collective-permute-start.4 = (bf16[4,4,4,64,128]{4,3,2,1,0:T(8,128)(2,1)}, bf16[4,4,4,64,128]{4,3,2,1,0:T(8,128)(2,1)}, u32[]{:S(2)}, u32[]{:S(2)}) collective-permute-start(bf16[4,4,4,64,128]{4,3,2,1,0:T(8,128)(2,1)} %get-tuple-element.30.own_hbm), channel_id=1, source_target_pairs={{8,16},{12,20},{16,8},{20,12},{9,17},{13,21},{17,9},{21,13},{10,18... | collective-permute-start | bytes 3145736 | tf_op jit(solution)/shard_map/ppermute | solution.py:427
  15.5 2.6 %collective-permute-start.7 = (bf16[4,4,4,64,128]{4,3,2,1,0:T(8,128)(2,1)}, bf16[4,4,4,64,128]{4,3,2,1,0:T(8,128)(2,1)}, u32[]{:S(2)}, u32[]{:S(2)}) collective-permute-start(bf16[4,4,4,64,128]{4,3,2,1,0:T(8,128)(2,1)} %get-tuple-element.33), channel_id=1, source_target_pairs={{0,8},{4,12},{8,24},{12,28},{16,0},{20,4},{24,16},{28,20},{1,9},{5... | collective-permute-start | bytes 3145736 | tf_op jit(solution)/shard_map/ppermute | solution.py:427
  18.1 2.9 %rotate_queries.1.query_ref = bf16[16,256,128]{2,1,0:T(8,128)(2,1)} custom-call(bf16[256,2048]{1,0:T(8,128)(2,1)} %query_ref.1, f32[1,2048]{1,0:T(1,128)} %bitcast.8, f32[256,128]{1,0:T(8,128)} %get-tuple-element.23.cos_ref, f32[256,128]{1,0:T(8,128)} %get-tuple-element.24.sin_ref), custom_call_target="tpu_custom_call" | custom-call | flops 1 | bytes 1 | tf_op jit(solution)/shard_map/rotate_queries/pallas_call | solution.py:200
  20.9 0.0 copy-start
  21.0 1.2 %copy-done = bf16[16,256,128]{2,1,0:T(8,128)(2,1)S(1)} copy-done((bf16[16,256,128]{2,1,0:T(8,128)(2,1)S(1)}, bf16[16,256,128]{2,1,0:T(8,128)(2,1)}, u32[]{:S(2)}) %copy-start) | copy-done | bytes 1048600
  22.2 4.4 %attend.3 = (f32[2,256,128]{2,1,0:T(8,128)S(1)}, f32[16,256,128]{2,1,0:T(8,128)S(1)}) custom-call(bf16[16,256,128]{2,1,0:T(8,128)(2,1)S(1)} %copy-done, s32[256,128]{1,0:T(8,128)S(1)} %copy-done.2, s32[16,128]{1,0:T(8,128)S(1)} %bitcast.5, bf16[2,2,256,128]{3,2,1,0:T(8,128)(2,1)S(1)} %copy-done.3, bf16[2,2,256,128]{3,2,1,0:T(8,128)(2,1)} %collective-permute-done.rest_1_), custom_call_target="tpu_custom_call" | custom-call | flops 1 | bytes 1 | tf_op jit(solution)/shard_map/attend/pallas_call | solution.py:285
  26.5 0.7 copy-done.8
  27.2 2.2 %collective-permute-done.3.rest_2_ = bf16[2,2,256,128]{3,2,1,0:T(8,128)(2,1)S(1)} collective-permute-done((bf16[2,2,256,128]{3,2,1,0:T(8,128)(2,1)}, bf16[2,2,256,128]{3,2,1,0:T(8,128)(2,1)S(1)}, u32[]{:S(2)}, u32[]{:S(2)}) %collective-permute-start.3) | collective-permute-done | bytes 262176 | tf_op jit(solution)/shard_map/ppermute | solution.py:413
  29.5 0.7 %copy-done.4 = bf16[2,2,256,128]{3,2,1,0:T(8,128)(2,1)} copy-done((bf16[2,2,256,128]{3,2,1,0:T(8,128)(2,1)}, bf16[2,2,256,128]{3,2,1,0:T(8,128)(2,1)S(1)}, u32[]{:S(2)}) %copy-start.4) | copy-done | bytes 262168
  30.2 0.0 collective-permute-done.1.rest_1_
  30.2 0.7 copy-done.6
  30.9 1.6 %collective-permute-start.9 = (bf16[4,4,4,64,128]{4,3,2,1,0:T(8,128)(2,1)}, bf16[4,4,4,64,128]{4,3,2,1,0:T(8,128)(2,1)}, u32[]{:S(2)}, u32[]{:S(2)}) collective-permute-start(bf16[4,4,4,64,128]{4,3,2,1,0:T(8,128)(2,1)} %get-tuple-element.40), channel_id=1, source_target_pairs={{0,4},{4,0},{8,20},{12,16},{16,12},{20,8},{24,28},{28,24},{1,5},{5... | collective-permute-start | bytes 3145736 | tf_op jit(solution)/shard_map/ppermute | solution.py:427
  32.5 2.5 %collective-permute-start.2 = (bf16[2,2,256,128]{3,2,1,0:T(8,128)(2,1)}, bf16[2,2,256,128]{3,2,1,0:T(8,128)(2,1)}, u32[]{:S(2)}, u32[]{:S(2)}) collective-permute-start(bf16[2,2,256,128]{3,2,1,0:T(8,128)(2,1)} %collective-permute-done.rest_1_), channel_id=1, source_target_pairs={{0,3},{1,2},{2,1},{3,0},{4,7},{5,6},{6,5},{7,4},{8,11},{9,10},{10,... | collective-permute-start | bytes 786440 | tf_op jit(solution)/shard_map/ppermute | solution.py:413
  35.0 2.7 %collective-permute-start.5 = (bf16[2,2,256,128]{3,2,1,0:T(8,128)(2,1)}, bf16[2,2,256,128]{3,2,1,0:T(8,128)(2,1)}, u32[]{:S(2)}, u32[]{:S(2)}) collective-permute-start(bf16[2,2,256,128]{3,2,1,0:T(8,128)(2,1)} %collective-permute-done.rest_1_), channel_id=1, source_target_pairs={{0,2},{1,3},{2,0},{3,1},{4,6},{5,7},{6,4},{7,5},{8,10},{9,11},{10,... | collective-permute-start | bytes 786440 | tf_op jit(solution)/shard_map/ppermute | solution.py:413
  37.7 5.5 %collective-permute-done.7.rest_1_ = bf16[4,4,4,64,128]{4,3,2,1,0:T(8,128)(2,1)} collective-permute-done((bf16[4,4,4,64,128]{4,3,2,1,0:T(8,128)(2,1)}, bf16[4,4,4,64,128]{4,3,2,1,0:T(8,128)(2,1)}, u32[]{:S(2)}, u32[]{:S(2)}) %collective-permute-start.7) | collective-permute-done | bytes 1048608 | tf_op jit(solution)/shard_map/ppermute | solution.py:427
  43.2 0.8 %collective-permute-start.8 = (bf16[2,2,256,128]{3,2,1,0:T(8,128)(2,1)}, bf16[2,2,256,128]{3,2,1,0:T(8,128)(2,1)}, u32[]{:S(2)}, u32[]{:S(2)}) collective-permute-start(bf16[2,2,256,128]{3,2,1,0:T(8,128)(2,1)} %collective-permute-done.rest_1_), channel_id=1, source_target_pairs={{0,1},{1,0},{2,3},{3,2},{4,5},{5,4},{6,7},{7,6},{8,9},{9,8},{10,11... | collective-permute-start | bytes 786440 | tf_op jit(solution)/shard_map/ppermute | solution.py:413
  44.0 3.6 %place.2.rest_2_ = bf16[1,1,8,8,4,64,128]{6,5,4,3,2,1,0:T(8,128)(2,1)} custom-call(s32[4,16]{1,0:T(4,128)} %page_ref.5, bf16[4,4,4,64,128]{4,3,2,1,0:T(8,128)(2,1)} %get-tuple-element.30.own_hbm, bf16[4,4,4,64,128]{4,3,2,1,0:T(8,128)(2,1)} %collective-permute-done.4.rest_0_, bf16[4,4,4,64,128]{4,3,2,1,0:T(8,128)(2,1)} %collective-permute-done.7.rest_1_), custom_call_target="tpu_custom_call" | custom-call | flops 1 | bytes 1 | tf_op jit(solution)/shard_map/place/pallas_call | solution.py:369
  47.6 0.9 %copy-done.5 = bf16[2,2,256,128]{3,2,1,0:T(8,128)(2,1)S(1)} copy-done((bf16[2,2,256,128]{3,2,1,0:T(8,128)(2,1)S(1)}, bf16[2,2,256,128]{3,2,1,0:T(8,128)(2,1)}, u32[]{:S(2)}) %copy-start.5) | copy-done | bytes 262168
  48.6 0.9 %copy-done.7 = bf16[2,2,256,128]{3,2,1,0:T(8,128)(2,1)S(1)} copy-done((bf16[2,2,256,128]{3,2,1,0:T(8,128)(2,1)S(1)}, bf16[2,2,256,128]{3,2,1,0:T(8,128)(2,1)}, u32[]{:S(2)}) %copy-start.7) | copy-done | bytes 262168
  49.5 0.9 %copy-done.9 = f32[2,256,128]{2,1,0:T(8,128)S(1)} copy-done((f32[2,256,128]{2,1,0:T(8,128)S(1)}, f32[2,256,128]{2,1,0:T(8,128)}, u32[]{:S(2)}) %copy-start.9) | copy-done | bytes 262168
  50.5 7.0 %attend.4 = (f32[2,256,128]{2,1,0:T(8,128)S(1)}, f32[16,256,128]{2,1,0:T(8,128)S(1)}) custom-call(bf16[16,256,128]{2,1,0:T(8,128)(2,1)S(1)} %copy-done.1, s32[256,128]{1,0:T(8,128)S(1)} %copy-done.2, s32[16,128]{1,0:T(8,128)S(1)} %bitcast.6, bf16[2,2,256,128]{3,2,1,0:T(8,128)(2,1)S(1)} %collective-permute-done.6.rest_0_, ...), custom_call_target="tpu_custom_call" | custom-call | flops 1 | bytes 1 | tf_op jit(solution)/shard_map/attend/pallas_call | solution.py:285
  57.5 2.2 %collective-permute-done.5.rest_1_ = bf16[2,2,256,128]{3,2,1,0:T(8,128)(2,1)} collective-permute-done((bf16[2,2,256,128]{3,2,1,0:T(8,128)(2,1)}, bf16[2,2,256,128]{3,2,1,0:T(8,128)(2,1)}, u32[]{:S(2)}, u32[]{:S(2)}) %collective-permute-start.5) | collective-permute-done | bytes 262176 | tf_op jit(solution)/shard_map/ppermute | solution.py:413
  59.7 8.7 %attend.5 = bf16[256,2048]{1,0:T(8,128)(2,1)} custom-call(bf16[16,256,128]{2,1,0:T(8,128)(2,1)S(1)} %copy-done.1, s32[256,128]{1,0:T(8,128)S(1)} %copy-done.2, s32[16,128]{1,0:T(8,128)S(1)} %bitcast.7, bf16[2,2,256,128]{3,2,1,0:T(8,128)(2,1)} %collective-permute-done.2.rest_0_, bf16[2,2,256,128]{3,2,1,0:T(8,128)(2,1)} %collective-permute-done.5.rest_1_, ...), custom_call_target="tpu_custom_call" | custom-call | flops 1 | bytes 1 | tf_op jit(solution)/shard_map/attend/pallas_call | solution.py:285
  68.4 2.8 %place.3 = bf16[1,1,8,8,4,64,128]{6,5,4,3,2,1,0:T(8,128)(2,1)} custom-call(s32[4,16]{1,0:T(4,128)} %page_ref.5, bf16[4,4,4,64,128]{4,3,2,1,0:T(8,128)(2,1)} %get-tuple-element.30.own_hbm, bf16[4,4,4,64,128]{4,3,2,1,0:T(8,128)(2,1)} %collective-permute-done.9.rest_0_, ...), custom_call_target="tpu_custom_call", output_to_operand_aliasing={{}: (4, {})} | custom-call | flops 1 | bytes 1 | tf_op jit(solution)/shard_map/place/pallas_call | solution.py:369
  (20 shorter events, 0.0 us)
Async XLA Ops:
  3.2 17.7 %copy-start.2 = (s32[256,128]{1,0:T(8,128)S(1)}, s32[256,128]{1,0:T(8,128)}, u32[]{:S(2)}) copy-start(s32[256,128]{1,0:T(8,128)} %get-tuple-element.25.qpos_ref) | copy-start | bytes 393220
  3.2 17.7 %copy-start.3 = (bf16[2,2,256,128]{3,2,1,0:T(8,128)(2,1)S(1)}, bf16[2,2,256,128]{3,2,1,0:T(8,128)(2,1)}, u32[]{:S(2)}) copy-start(bf16[2,2,256,128]{3,2,1,0:T(8,128)(2,1)} %get-tuple-element.26.rest_0_.kv_hbm) | copy-start | bytes 786436
  3.2 17.7 %copy-start.10 = (s32[2048]{0:T(1024)S(1)}, s32[2048]{0:T(1024)}, u32[]{:S(2)}) copy-start(s32[2048]{0:T(1024)} %param.18) | copy-start | bytes 24580
  3.3 10.6 %collective-permute-start = (bf16[2,2,256,128]{3,2,1,0:T(8,128)(2,1)}, bf16[2,2,256,128]{3,2,1,0:T(8,128)(2,1)}, u32[]{:S(2)}, u32[]{:S(2)}) collective-permute-start(bf16[2,2,256,128]{3,2,1,0:T(8,128)(2,1)} %get-tuple-element.26.rest_0_.kv_hbm), channel_id=1, source_target_pairs={{0,16},{16,0},{1,17},{17,1},{2,18},{18,2},{3,19},{19,3},{4,20},{20... | collective-permute-start | bytes 786440 | tf_op jit(solution)/shard_map/ppermute | solution.py:413
  6.3 20.9 %collective-permute-start.6 = (bf16[2,2,256,128]{3,2,1,0:T(8,128)(2,1)}, bf16[2,2,256,128]{3,2,1,0:T(8,128)(2,1)S(1)}, u32[]{:S(2)}, u32[]{:S(2)}) collective-permute-start(bf16[2,2,256,128]{3,2,1,0:T(8,128)(2,1)} %get-tuple-element.26.rest_0_.kv_hbm), channel_id=1, source_target_pairs={{0,1},{1,0},{2,3},{3,2},{4,5},{5,4},{6,7},{7,6},{8,9},{9,8},{10,11... | collective-permute-start | bytes 786440 | tf_op jit(solution)/shard_map/ppermute | solution.py:413
  7.9 21.6 %collective-permute-start.3 = (bf16[2,2,256,128]{3,2,1,0:T(8,128)(2,1)}, bf16[2,2,256,128]{3,2,1,0:T(8,128)(2,1)S(1)}, u32[]{:S(2)}, u32[]{:S(2)}) collective-permute-start(bf16[2,2,256,128]{3,2,1,0:T(8,128)(2,1)} %get-tuple-element.26.rest_0_.kv_hbm), channel_id=1, source_target_pairs={{0,2},{1,3},{2,0},{3,1},{4,6},{5,7},{6,4},{7,5},{8,10},{9,11},{10,... | collective-permute-start | bytes 786440 | tf_op jit(solution)/shard_map/ppermute | solution.py:413
  10.5 19.7 %collective-permute-start.1 = (bf16[2,2,256,128]{3,2,1,0:T(8,128)(2,1)}, bf16[2,2,256,128]{3,2,1,0:T(8,128)(2,1)S(1)}, u32[]{:S(2)}, u32[]{:S(2)}) collective-permute-start(bf16[2,2,256,128]{3,2,1,0:T(8,128)(2,1)} %get-tuple-element.26.rest_0_.kv_hbm), channel_id=1, source_target_pairs={{0,3},{1,2},{2,1},{3,0},{4,7},{5,6},{6,5},{7,4},{8,11},{9,10},{10,... | collective-permute-start | bytes 786440 | tf_op jit(solution)/shard_map/ppermute | solution.py:413
  13.9 21.1 %collective-permute-start.4 = (bf16[4,4,4,64,128]{4,3,2,1,0:T(8,128)(2,1)}, bf16[4,4,4,64,128]{4,3,2,1,0:T(8,128)(2,1)}, u32[]{:S(2)}, u32[]{:S(2)}) collective-permute-start(bf16[4,4,4,64,128]{4,3,2,1,0:T(8,128)(2,1)} %get-tuple-element.30.own_hbm), channel_id=1, source_target_pairs={{8,16},{12,20},{16,8},{20,12},{9,17},{13,21},{17,9},{21,13},{10,18... | collective-permute-start | bytes 3145736 | tf_op jit(solution)/shard_map/ppermute | solution.py:427
  15.5 27.7 %collective-permute-start.7 = (bf16[4,4,4,64,128]{4,3,2,1,0:T(8,128)(2,1)}, bf16[4,4,4,64,128]{4,3,2,1,0:T(8,128)(2,1)}, u32[]{:S(2)}, u32[]{:S(2)}) collective-permute-start(bf16[4,4,4,64,128]{4,3,2,1,0:T(8,128)(2,1)} %get-tuple-element.33), channel_id=1, source_target_pairs={{0,8},{4,12},{8,24},{12,28},{16,0},{20,4},{24,16},{28,20},{1,9},{5... | collective-permute-start | bytes 3145736 | tf_op jit(solution)/shard_map/ppermute | solution.py:427
  20.9 1.2 %copy-start = (bf16[16,256,128]{2,1,0:T(8,128)(2,1)S(1)}, bf16[16,256,128]{2,1,0:T(8,128)(2,1)}, u32[]{:S(2)}) copy-start(bf16[16,256,128]{2,1,0:T(8,128)(2,1)} %rotate_queries.1.query_ref) | copy-start | bytes 3145732
  26.5 0.7 copy-start.8
  29.5 0.7 %copy-start.4 = (bf16[2,2,256,128]{3,2,1,0:T(8,128)(2,1)}, bf16[2,2,256,128]{3,2,1,0:T(8,128)(2,1)S(1)}, u32[]{:S(2)}) copy-start(bf16[2,2,256,128]{3,2,1,0:T(8,128)(2,1)S(1)} %collective-permute-done.3.rest_2_) | copy-start | bytes 786436
  30.2 0.7 copy-start.6
  30.9 16.7 %copy-start.1 = (bf16[16,256,128]{2,1,0:T(8,128)(2,1)S(1)}, bf16[16,256,128]{2,1,0:T(8,128)(2,1)}, u32[]{:S(2)}) copy-start(bf16[16,256,128]{2,1,0:T(8,128)(2,1)} %rotate_queries.1.query_ref) | copy-start | bytes 3145732
  30.9 37.5 %collective-permute-start.10 = (bf16[4,4,4,64,128]{4,3,2,1,0:T(8,128)(2,1)}, bf16[4,4,4,64,128]{4,3,2,1,0:T(8,128)(2,1)}, u32[]{:S(2)}, u32[]{:S(2)}) collective-permute-start(bf16[4,4,4,64,128]{4,3,2,1,0:T(8,128)(2,1)} %get-tuple-element.42), channel_id=1, source_target_pairs={{0,12},{4,8},{8,28},{12,24},{16,4},{20,0},{24,20},{28,16},{1,13},{... | collective-permute-start | bytes 3145736 | tf_op jit(solution)/shard_map/ppermute | solution.py:427
  30.9 37.5 %collective-permute-start.9 = (bf16[4,4,4,64,128]{4,3,2,1,0:T(8,128)(2,1)}, bf16[4,4,4,64,128]{4,3,2,1,0:T(8,128)(2,1)}, u32[]{:S(2)}, u32[]{:S(2)}) collective-permute-start(bf16[4,4,4,64,128]{4,3,2,1,0:T(8,128)(2,1)} %get-tuple-element.40), channel_id=1, source_target_pairs={{0,4},{4,0},{8,20},{12,16},{16,12},{20,8},{24,28},{28,24},{1,5},{5... | collective-permute-start | bytes 3145736 | tf_op jit(solution)/shard_map/ppermute | solution.py:427
  32.5 24.9 %collective-permute-start.2 = (bf16[2,2,256,128]{3,2,1,0:T(8,128)(2,1)}, bf16[2,2,256,128]{3,2,1,0:T(8,128)(2,1)}, u32[]{:S(2)}, u32[]{:S(2)}) collective-permute-start(bf16[2,2,256,128]{3,2,1,0:T(8,128)(2,1)} %collective-permute-done.rest_1_), channel_id=1, source_target_pairs={{0,3},{1,2},{2,1},{3,0},{4,7},{5,6},{6,5},{7,4},{8,11},{9,10},{10,... | collective-permute-start | bytes 786440 | tf_op jit(solution)/shard_map/ppermute | solution.py:413
  35.0 24.7 %collective-permute-start.5 = (bf16[2,2,256,128]{3,2,1,0:T(8,128)(2,1)}, bf16[2,2,256,128]{3,2,1,0:T(8,128)(2,1)}, u32[]{:S(2)}, u32[]{:S(2)}) collective-permute-start(bf16[2,2,256,128]{3,2,1,0:T(8,128)(2,1)} %collective-permute-done.rest_1_), channel_id=1, source_target_pairs={{0,2},{1,3},{2,0},{3,1},{4,6},{5,7},{6,4},{7,5},{8,10},{9,11},{10,... | collective-permute-start | bytes 786440 | tf_op jit(solution)/shard_map/ppermute | solution.py:413
  43.2 16.5 %collective-permute-start.8 = (bf16[2,2,256,128]{3,2,1,0:T(8,128)(2,1)}, bf16[2,2,256,128]{3,2,1,0:T(8,128)(2,1)}, u32[]{:S(2)}, u32[]{:S(2)}) collective-permute-start(bf16[2,2,256,128]{3,2,1,0:T(8,128)(2,1)} %collective-permute-done.rest_1_), channel_id=1, source_target_pairs={{0,1},{1,0},{2,3},{3,2},{4,5},{5,4},{6,7},{7,6},{8,9},{9,8},{10,11... | collective-permute-start | bytes 786440 | tf_op jit(solution)/shard_map/ppermute | solution.py:413
  47.6 1.0 %copy-start.5 = (bf16[2,2,256,128]{3,2,1,0:T(8,128)(2,1)S(1)}, bf16[2,2,256,128]{3,2,1,0:T(8,128)(2,1)}, u32[]{:S(2)}) copy-start(bf16[2,2,256,128]{3,2,1,0:T(8,128)(2,1)} %copy-done.4) | copy-start | bytes 786436
  48.6 0.9 %copy-start.7 = (bf16[2,2,256,128]{3,2,1,0:T(8,128)(2,1)S(1)}, bf16[2,2,256,128]{3,2,1,0:T(8,128)(2,1)}, u32[]{:S(2)}) copy-start(bf16[2,2,256,128]{3,2,1,0:T(8,128)(2,1)} %copy-done.6) | copy-start | bytes 786436
  49.5 0.9 %copy-start.9 = (f32[2,256,128]{2,1,0:T(8,128)S(1)}, f32[2,256,128]{2,1,0:T(8,128)}, u32[]{:S(2)}) copy-start(f32[2,256,128]{2,1,0:T(8,128)} %copy-done.8) | copy-start | bytes 786436

commit v4 on v3

--- a/solution.py
+++ b/solution.py
@@ -439,7 +439,7 @@
     far = []
     for r in hops[1:]:
         for s in range(1, pre_size):
-            wait = (own[r], state[0]) if r == hops[1] else (own[r], arrived[order[0]])
+            wait = (own[1], state[0]) if r == hops[1] else (own[r], arrived[order[0]])
             far.append(((s, r), swap(after(near[s], *wait), "rep", rep_size, r)))
     for j in order[3:]:
         hand_over(j, near[-1], state[0], own[1], own[hops[-1]])

time: 71.9 us -> 71.1 us (0.989)
  the two profiles are of different devices: /device:TPU:0 before, /device:TPU:1 now
where the time goes in v4:
time: 71.1 us; the launch traced here: 70.3 us
  Pallas kernels  35 us (49%)
  starting transfers between devices  15.7 us (22%)
  waiting for transfers between devices  12.6 us (18%)
  local copies, waits for them, and re-layouts  6.21 us (9%)
  between operations  0.77 us (1%)
    pallas_call x3, Pallas kernels, attend(): pl.pallas_call(functools.partial(attend_kernel, moves, rep_size, first, l...  20 us
    ppermute x7, waiting for transfers between devices, shards(): lax.ppermute(value, axis, [(i, i ^ hop) for i in range(size)])  11.2 us
    ppermute x7, starting transfers between devices, shards(): lax.ppermute(value, axis, [(i, i ^ hop) for i in range(size)])  9.34 us
    pallas_call x2, Pallas kernels, place(): pl.pallas_call(functools.partial(place_kernel, dims, here, rest_j), out_s...  6.41 us
    ppermute x4, starting transfers between devices, hand_over(): arrived[j] = lax.ppermute(after(sends[j], *before), ('pre', 'dec'), route)  6.37 us
    unnamed x22, local copies, waits for them, and re-layouts  6.21 us
    pallas_call x1, Pallas kernels, pack(): pl.pallas_call(functools.partial(pack_kernel, dims), out_shape=[jax.Shape...  3.17 us
    pallas_call x1, Pallas kernels, rotate_queries(): pl.pallas_call(query_kernel, out_shape=jax.ShapeDtypeStruct((columns // H...  2.86 us
  transfers between devices with their start and end apart: 11, of which 3 were waited for; matrix products, arithmetic and copies ran while one was open for 0% of the time, Pallas kernels for 42%

profile of v4, /device:TPU:1, one launch (start us, length us, event | category | flops | bytes accessed | tf_op | source)
XLA Modules:
  0.0 70.3 jit_solution(16673906221233259842)
XLA Ops:
  0.6 2.6 %turn.1 = (bf16[2,2,256,128]{3,2,1,0:T(8,128)(2,1)}, f32[256,128]{1,0:T(8,128)}, f32[256,128]{1,0:T(8,128)}, s32[256,128]{1,0:T(8,128)}) custom-call(s32[16,128]{1,0:T(8,128)} %bitcast.4, f32[1,128]{1,0:T(1,128)} %constant.2.clone.freq_ref, f32[1,1024]{1,0:T(1,128)} %bitcast.9, f32[1,1024]{1,0:T(1,128)} %bitcast.10, bf16[256,1024]{1,0:T(8,128)(2,1)} %keys_hbm.1, ...), custom_call_target="tpu_custom_call" | custom-call | flops 1 | bytes 1 | tf_op jit(solution)/shard_map/turn/pallas_call | solution.py:86
  3.2 0.0 copy-start.10
  3.3 2.1 %collective-permute-start = (bf16[2,2,256,128]{3,2,1,0:T(8,128)(2,1)}, bf16[2,2,256,128]{3,2,1,0:T(8,128)(2,1)}, u32[]{:S(2)}, u32[]{:S(2)}) collective-permute-start(bf16[2,2,256,128]{3,2,1,0:T(8,128)(2,1)} %get-tuple-element.26.rest_0_.kv_hbm), channel_id=1, source_target_pairs={{0,16},{16,0},{1,17},{17,1},{2,18},{18,2},{3,19},{19,3},{4,20},{20... | collective-permute-start | bytes 786440 | tf_op jit(solution)/shard_map/ppermute | solution.py:413
  5.4 3.3 %collective-permute-start.8 = (bf16[2,2,256,128]{3,2,1,0:T(8,128)(2,1)}, bf16[2,2,256,128]{3,2,1,0:T(8,128)(2,1)S(1)}, u32[]{:S(2)}, u32[]{:S(2)}) collective-permute-start(bf16[2,2,256,128]{3,2,1,0:T(8,128)(2,1)} %get-tuple-element.26.rest_0_.kv_hbm), channel_id=1, source_target_pairs={{0,3},{1,2},{2,1},{3,0},{4,7},{5,6},{6,5},{7,4},{8,11},{9,10},{10,... | collective-permute-start | bytes 786440 | tf_op jit(solution)/shard_map/ppermute | solution.py:413
  8.7 0.0 collective-permute-start.3
  8.7 0.3 collective-permute-start.1
  9.0 3.2 %pack.1 = (bf16[4,4,4,64,128]{4,3,2,1,0:T(8,128)(2,1)}, bf16[4,4,4,64,128]{4,3,2,1,0:T(8,128)(2,1)}, bf16[4,4,4,64,128]{4,3,2,1,0:T(8,128)(2,1)}, bf16[4,4,4,64,128]{4,3,2,1,0:T(8,128)(2,1)}) custom-call(s32[4,16]{1,0:T(4,128)} %page_ref.5, s32[32]{0:T(128)} %lengths_ref.1, s32[32]{0:T(128)} %replica_ref.1, ...), custom_call_target="tpu_custom_call" | custom-call | flops 1 | bytes 1 | tf_op jit(solution)/shard_map/pack/pallas_call | solution.py:170
  12.2 0.0 collective-permute-done.rest_1_
  12.2 1.7 %collective-permute-start.4 = (bf16[4,4,4,64,128]{4,3,2,1,0:T(8,128)(2,1)}, bf16[4,4,4,64,128]{4,3,2,1,0:T(8,128)(2,1)}, u32[]{:S(2)}, u32[]{:S(2)}) collective-permute-start(bf16[4,4,4,64,128]{4,3,2,1,0:T(8,128)(2,1)} %get-tuple-element.30.own_hbm), channel_id=1, source_target_pairs={{8,16},{12,20},{16,8},{20,12},{9,17},{13,21},{17,9},{21,13},{10,18... | collective-permute-start | bytes 3145736 | tf_op jit(solution)/shard_map/ppermute | solution.py:427
  13.8 2.2 %collective-permute-start.6 = (bf16[4,4,4,64,128]{4,3,2,1,0:T(8,128)(2,1)}, bf16[4,4,4,64,128]{4,3,2,1,0:T(8,128)(2,1)}, u32[]{:S(2)}, u32[]{:S(2)}) collective-permute-start(bf16[4,4,4,64,128]{4,3,2,1,0:T(8,128)(2,1)} %get-tuple-element.33), channel_id=1, source_target_pairs={{0,8},{4,12},{8,24},{12,28},{16,0},{20,4},{24,16},{28,20},{1,9},{5... | collective-permute-start | bytes 3145736 | tf_op jit(solution)/shard_map/ppermute | solution.py:427
  16.0 2.9 %rotate_queries.1.query_ref = bf16[16,256,128]{2,1,0:T(8,128)(2,1)} custom-call(bf16[256,2048]{1,0:T(8,128)(2,1)} %query_ref.1, f32[1,2048]{1,0:T(1,128)} %bitcast.8, f32[256,128]{1,0:T(8,128)} %get-tuple-element.23.cos_ref, f32[256,128]{1,0:T(8,128)} %get-tuple-element.24.sin_ref), custom_call_target="tpu_custom_call" | custom-call | flops 1 | bytes 1 | tf_op jit(solution)/shard_map/rotate_queries/pallas_call | solution.py:200
  18.9 0.0 copy-start
  18.9 1.2 %copy-done = bf16[16,256,128]{2,1,0:T(8,128)(2,1)S(1)} copy-done((bf16[16,256,128]{2,1,0:T(8,128)(2,1)S(1)}, bf16[16,256,128]{2,1,0:T(8,128)(2,1)}, u32[]{:S(2)}) %copy-start) | copy-done | bytes 1048600
  20.1 4.3 %attend.3 = (f32[2,256,128]{2,1,0:T(8,128)S(1)}, f32[16,256,128]{2,1,0:T(8,128)S(1)}) custom-call(bf16[16,256,128]{2,1,0:T(8,128)(2,1)S(1)} %copy-done, s32[256,128]{1,0:T(8,128)S(1)} %copy-done.2, s32[16,128]{1,0:T(8,128)S(1)} %bitcast.5, bf16[2,2,256,128]{3,2,1,0:T(8,128)(2,1)S(1)} %copy-done.3, bf16[2,2,256,128]{3,2,1,0:T(8,128)(2,1)} %collective-permute-done.rest_1_), custom_call_target="tpu_custom_call" | custom-call | flops 1 | bytes 1 | tf_op jit(solution)/shard_map/attend/pallas_call | solution.py:285
  24.5 0.7 copy-done.8
  25.2 5.6 %collective-permute-done.3.rest_2_ = bf16[2,2,256,128]{3,2,1,0:T(8,128)(2,1)S(1)} collective-permute-done((bf16[2,2,256,128]{3,2,1,0:T(8,128)(2,1)}, bf16[2,2,256,128]{3,2,1,0:T(8,128)(2,1)S(1)}, u32[]{:S(2)}, u32[]{:S(2)}) %collective-permute-start.3) | collective-permute-done | bytes 262176 | tf_op jit(solution)/shard_map/ppermute | solution.py:413
  30.8 0.7 %copy-done.4 = bf16[2,2,256,128]{3,2,1,0:T(8,128)(2,1)} copy-done((bf16[2,2,256,128]{3,2,1,0:T(8,128)(2,1)}, bf16[2,2,256,128]{3,2,1,0:T(8,128)(2,1)S(1)}, u32[]{:S(2)}) %copy-start.4) | copy-done | bytes 262168
  31.5 0.0 collective-permute-done.1.rest_0_
  31.5 0.7 copy-done.6
  32.2 2.5 %collective-permute-start.10 = (bf16[4,4,4,64,128]{4,3,2,1,0:T(8,128)(2,1)}, bf16[4,4,4,64,128]{4,3,2,1,0:T(8,128)(2,1)}, u32[]{:S(2)}, u32[]{:S(2)}) collective-permute-start(bf16[4,4,4,64,128]{4,3,2,1,0:T(8,128)(2,1)} %get-tuple-element.42), channel_id=1, source_target_pairs={{0,12},{4,8},{8,28},{12,24},{16,4},{20,0},{24,20},{28,16},{1,13},{... | collective-permute-start | bytes 3145736 | tf_op jit(solution)/shard_map/ppermute | solution.py:427
  34.7 0.0 collective-permute-start.9
  34.7 2.2 %collective-permute-start.2 = (bf16[2,2,256,128]{3,2,1,0:T(8,128)(2,1)}, bf16[2,2,256,128]{3,2,1,0:T(8,128)(2,1)}, u32[]{:S(2)}, u32[]{:S(2)}) collective-permute-start(bf16[2,2,256,128]{3,2,1,0:T(8,128)(2,1)} %collective-permute-done.rest_1_), channel_id=1, source_target_pairs={{0,3},{1,2},{2,1},{3,0},{4,7},{5,6},{6,5},{7,4},{8,11},{9,10},{10,... | collective-permute-start | bytes 786440 | tf_op jit(solution)/shard_map/ppermute | solution.py:413
  36.9 1.4 %collective-permute-done.6.rest_1_ = bf16[4,4,4,64,128]{4,3,2,1,0:T(8,128)(2,1)} collective-permute-done((bf16[4,4,4,64,128]{4,3,2,1,0:T(8,128)(2,1)}, bf16[4,4,4,64,128]{4,3,2,1,0:T(8,128)(2,1)}, u32[]{:S(2)}, u32[]{:S(2)}) %collective-permute-start.6) | collective-permute-done | bytes 1048608 | tf_op jit(solution)/shard_map/ppermute | solution.py:427
  38.3 1.4 %collective-permute-start.7 = (bf16[2,2,256,128]{3,2,1,0:T(8,128)(2,1)}, bf16[2,2,256,128]{3,2,1,0:T(8,128)(2,1)}, u32[]{:S(2)}, u32[]{:S(2)}) collective-permute-start(bf16[2,2,256,128]{3,2,1,0:T(8,128)(2,1)} %collective-permute-done.rest_1_), channel_id=1, source_target_pairs={{0,1},{1,0},{2,3},{3,2},{4,5},{5,4},{6,7},{7,6},{8,9},{9,8},{10,11... | collective-permute-start | bytes 786440 | tf_op jit(solution)/shard_map/ppermute | solution.py:413
  39.7 3.3 %place.2.rest_2_ = bf16[1,1,8,8,4,64,128]{6,5,4,3,2,1,0:T(8,128)(2,1)} custom-call(s32[4,16]{1,0:T(4,128)} %page_ref.5, bf16[4,4,4,64,128]{4,3,2,1,0:T(8,128)(2,1)} %get-tuple-element.30.own_hbm, bf16[4,4,4,64,128]{4,3,2,1,0:T(8,128)(2,1)} %collective-permute-done.4.rest_0_, bf16[4,4,4,64,128]{4,3,2,1,0:T(8,128)(2,1)} %collective-permute-done.6.rest_1_), custom_call_target="tpu_custom_call" | custom-call | flops 1 | bytes 1 | tf_op jit(solution)/shard_map/place/pallas_call | solution.py:369
  43.0 0.9 %copy-done.5 = bf16[2,2,256,128]{3,2,1,0:T(8,128)(2,1)S(1)} copy-done((bf16[2,2,256,128]{3,2,1,0:T(8,128)(2,1)S(1)}, bf16[2,2,256,128]{3,2,1,0:T(8,128)(2,1)}, u32[]{:S(2)}) %copy-start.5) | copy-done | bytes 262168
  44.0 0.9 %copy-done.7 = bf16[2,2,256,128]{3,2,1,0:T(8,128)(2,1)S(1)} copy-done((bf16[2,2,256,128]{3,2,1,0:T(8,128)(2,1)S(1)}, bf16[2,2,256,128]{3,2,1,0:T(8,128)(2,1)}, u32[]{:S(2)}) %copy-start.7) | copy-done | bytes 262168
  44.9 0.9 %copy-done.9 = f32[2,256,128]{2,1,0:T(8,128)S(1)} copy-done((f32[2,256,128]{2,1,0:T(8,128)S(1)}, f32[2,256,128]{2,1,0:T(8,128)}, u32[]{:S(2)}) %copy-start.9) | copy-done | bytes 262168
  45.9 7.0 %attend.4 = (f32[2,256,128]{2,1,0:T(8,128)S(1)}, f32[16,256,128]{2,1,0:T(8,128)S(1)}) custom-call(bf16[16,256,128]{2,1,0:T(8,128)(2,1)S(1)} %copy-done.1, s32[256,128]{1,0:T(8,128)S(1)} %copy-done.2, s32[16,128]{1,0:T(8,128)S(1)} %bitcast.6, bf16[2,2,256,128]{3,2,1,0:T(8,128)(2,1)S(1)} %copy-done.7, ...), custom_call_target="tpu_custom_call" | custom-call | flops 1 | bytes 1 | tf_op jit(solution)/shard_map/attend/pallas_call | solution.py:285
  52.9 5.6 %collective-permute-done.5.rest_1_ = bf16[2,2,256,128]{3,2,1,0:T(8,128)(2,1)} collective-permute-done((bf16[2,2,256,128]{3,2,1,0:T(8,128)(2,1)}, bf16[2,2,256,128]{3,2,1,0:T(8,128)(2,1)}, u32[]{:S(2)}, u32[]{:S(2)}) %collective-permute-start.5) | collective-permute-done | bytes 262176 | tf_op jit(solution)/shard_map/ppermute | solution.py:413
  58.5 8.7 %attend.5 = bf16[256,2048]{1,0:T(8,128)(2,1)} custom-call(bf16[16,256,128]{2,1,0:T(8,128)(2,1)S(1)} %copy-done.1, s32[256,128]{1,0:T(8,128)S(1)} %copy-done.2, s32[16,128]{1,0:T(8,128)S(1)} %bitcast.7, bf16[2,2,256,128]{3,2,1,0:T(8,128)(2,1)} %collective-permute-done.2.rest_0_, bf16[2,2,256,128]{3,2,1,0:T(8,128)(2,1)} %collective-permute-done.5.rest_1_, ...), custom_call_target="tpu_custom_call" | custom-call | flops 1 | bytes 1 | tf_op jit(solution)/shard_map/attend/pallas_call | solution.py:285
  67.1 3.1 %place.3 = bf16[1,1,8,8,4,64,128]{6,5,4,3,2,1,0:T(8,128)(2,1)} custom-call(s32[4,16]{1,0:T(4,128)} %page_ref.5, bf16[4,4,4,64,128]{4,3,2,1,0:T(8,128)(2,1)} %get-tuple-element.30.own_hbm, bf16[4,4,4,64,128]{4,3,2,1,0:T(8,128)(2,1)} %collective-permute-done.9.rest_0_, ...), custom_call_target="tpu_custom_call", output_to_operand_aliasing={{}: (4, {})} | custom-call | flops 1 | bytes 1 | tf_op jit(solution)/shard_map/place/pallas_call | solution.py:369
  (20 shorter events, 0.0 us)
Async XLA Ops:
  3.2 15.7 %copy-start.2 = (s32[256,128]{1,0:T(8,128)S(1)}, s32[256,128]{1,0:T(8,128)}, u32[]{:S(2)}) copy-start(s32[256,128]{1,0:T(8,128)} %get-tuple-element.25.qpos_ref) | copy-start | bytes 393220
  3.2 15.7 %copy-start.3 = (bf16[2,2,256,128]{3,2,1,0:T(8,128)(2,1)S(1)}, bf16[2,2,256,128]{3,2,1,0:T(8,128)(2,1)}, u32[]{:S(2)}) copy-start(bf16[2,2,256,128]{3,2,1,0:T(8,128)(2,1)} %get-tuple-element.26.rest_0_.kv_hbm) | copy-start | bytes 786436
  3.2 15.6 %copy-start.10 = (s32[2048]{0:T(1024)S(1)}, s32[2048]{0:T(1024)}, u32[]{:S(2)}) copy-start(s32[2048]{0:T(1024)} %param.18) | copy-start | bytes 24580
  3.3 8.9 %collective-permute-start = (bf16[2,2,256,128]{3,2,1,0:T(8,128)(2,1)}, bf16[2,2,256,128]{3,2,1,0:T(8,128)(2,1)}, u32[]{:S(2)}, u32[]{:S(2)}) collective-permute-start(bf16[2,2,256,128]{3,2,1,0:T(8,128)(2,1)} %get-tuple-element.26.rest_0_.kv_hbm), channel_id=1, source_target_pairs={{0,16},{16,0},{1,17},{17,1},{2,18},{18,2},{3,19},{19,3},{4,20},{20... | collective-permute-start | bytes 786440 | tf_op jit(solution)/shard_map/ppermute | solution.py:413
  5.4 19.8 %collective-permute-start.8 = (bf16[2,2,256,128]{3,2,1,0:T(8,128)(2,1)}, bf16[2,2,256,128]{3,2,1,0:T(8,128)(2,1)S(1)}, u32[]{:S(2)}, u32[]{:S(2)}) collective-permute-start(bf16[2,2,256,128]{3,2,1,0:T(8,128)(2,1)} %get-tuple-element.26.rest_0_.kv_hbm), channel_id=1, source_target_pairs={{0,3},{1,2},{2,1},{3,0},{4,7},{5,6},{6,5},{7,4},{8,11},{9,10},{10,... | collective-permute-start | bytes 786440 | tf_op jit(solution)/shard_map/ppermute | solution.py:413
  8.7 22.0 %collective-permute-start.3 = (bf16[2,2,256,128]{3,2,1,0:T(8,128)(2,1)}, bf16[2,2,256,128]{3,2,1,0:T(8,128)(2,1)S(1)}, u32[]{:S(2)}, u32[]{:S(2)}) collective-permute-start(bf16[2,2,256,128]{3,2,1,0:T(8,128)(2,1)} %get-tuple-element.26.rest_0_.kv_hbm), channel_id=1, source_target_pairs={{0,2},{1,3},{2,0},{3,1},{4,6},{5,7},{6,4},{7,5},{8,10},{9,11},{10,... | collective-permute-start | bytes 786440 | tf_op jit(solution)/shard_map/ppermute | solution.py:413
  8.7 22.8 %collective-permute-start.1 = (bf16[2,2,256,128]{3,2,1,0:T(8,128)(2,1)}, bf16[2,2,256,128]{3,2,1,0:T(8,128)(2,1)S(1)}, u32[]{:S(2)}, u32[]{:S(2)}) collective-permute-start(bf16[2,2,256,128]{3,2,1,0:T(8,128)(2,1)} %get-tuple-element.26.rest_0_.kv_hbm), channel_id=1, source_target_pairs={{0,1},{1,0},{2,3},{3,2},{4,5},{5,4},{6,7},{7,6},{8,9},{9,8},{10,11... | collective-permute-start | bytes 786440 | tf_op jit(solution)/shard_map/ppermute | solution.py:413
  12.2 24.8 %collective-permute-start.4 = (bf16[4,4,4,64,128]{4,3,2,1,0:T(8,128)(2,1)}, bf16[4,4,4,64,128]{4,3,2,1,0:T(8,128)(2,1)}, u32[]{:S(2)}, u32[]{:S(2)}) collective-permute-start(bf16[4,4,4,64,128]{4,3,2,1,0:T(8,128)(2,1)} %get-tuple-element.30.own_hbm), channel_id=1, source_target_pairs={{8,16},{12,20},{16,8},{20,12},{9,17},{13,21},{17,9},{21,13},{10,18... | collective-permute-start | bytes 3145736 | tf_op jit(solution)/shard_map/ppermute | solution.py:427
  13.8 24.5 %collective-permute-start.6 = (bf16[4,4,4,64,128]{4,3,2,1,0:T(8,128)(2,1)}, bf16[4,4,4,64,128]{4,3,2,1,0:T(8,128)(2,1)}, u32[]{:S(2)}, u32[]{:S(2)}) collective-permute-start(bf16[4,4,4,64,128]{4,3,2,1,0:T(8,128)(2,1)} %get-tuple-element.33), channel_id=1, source_target_pairs={{0,8},{4,12},{8,24},{12,28},{16,0},{20,4},{24,16},{28,20},{1,9},{5... | collective-permute-start | bytes 3145736 | tf_op jit(solution)/shard_map/ppermute | solution.py:427
  18.9 1.2 %copy-start = (bf16[16,256,128]{2,1,0:T(8,128)(2,1)S(1)}, bf16[16,256,128]{2,1,0:T(8,128)(2,1)}, u32[]{:S(2)}) copy-start(bf16[16,256,128]{2,1,0:T(8,128)(2,1)} %rotate_queries.1.query_ref) | copy-start | bytes 3145732
  24.5 0.7 copy-start.8
  30.8 0.7 %copy-start.4 = (bf16[2,2,256,128]{3,2,1,0:T(8,128)(2,1)}, bf16[2,2,256,128]{3,2,1,0:T(8,128)(2,1)S(1)}, u32[]{:S(2)}) copy-start(bf16[2,2,256,128]{3,2,1,0:T(8,128)(2,1)S(1)} %collective-permute-done.3.rest_2_) | copy-start | bytes 786436
  31.5 0.7 copy-start.6
  32.2 10.8 %copy-start.1 = (bf16[16,256,128]{2,1,0:T(8,128)(2,1)S(1)}, bf16[16,256,128]{2,1,0:T(8,128)(2,1)}, u32[]{:S(2)}) copy-start(bf16[16,256,128]{2,1,0:T(8,128)(2,1)} %rotate_queries.1.query_ref) | copy-start | bytes 3145732
  32.2 34.9 %collective-permute-start.10 = (bf16[4,4,4,64,128]{4,3,2,1,0:T(8,128)(2,1)}, bf16[4,4,4,64,128]{4,3,2,1,0:T(8,128)(2,1)}, u32[]{:S(2)}, u32[]{:S(2)}) collective-permute-start(bf16[4,4,4,64,128]{4,3,2,1,0:T(8,128)(2,1)} %get-tuple-element.42), channel_id=1, source_target_pairs={{0,12},{4,8},{8,28},{12,24},{16,4},{20,0},{24,20},{28,16},{1,13},{... | collective-permute-start | bytes 3145736 | tf_op jit(solution)/shard_map/ppermute | solution.py:427
  34.7 32.4 %collective-permute-start.9 = (bf16[4,4,4,64,128]{4,3,2,1,0:T(8,128)(2,1)}, bf16[4,4,4,64,128]{4,3,2,1,0:T(8,128)(2,1)}, u32[]{:S(2)}, u32[]{:S(2)}) collective-permute-start(bf16[4,4,4,64,128]{4,3,2,1,0:T(8,128)(2,1)} %get-tuple-element.40), channel_id=1, source_target_pairs={{0,4},{4,0},{8,20},{12,16},{16,12},{20,8},{24,28},{28,24},{1,5},{5... | collective-permute-start | bytes 3145736 | tf_op jit(solution)/shard_map/ppermute | solution.py:427
  34.7 18.1 %collective-permute-start.2 = (bf16[2,2,256,128]{3,2,1,0:T(8,128)(2,1)}, bf16[2,2,256,128]{3,2,1,0:T(8,128)(2,1)}, u32[]{:S(2)}, u32[]{:S(2)}) collective-permute-start(bf16[2,2,256,128]{3,2,1,0:T(8,128)(2,1)} %collective-permute-done.rest_1_), channel_id=1, source_target_pairs={{0,3},{1,2},{2,1},{3,0},{4,7},{5,6},{6,5},{7,4},{8,11},{9,10},{10,... | collective-permute-start | bytes 786440 | tf_op jit(solution)/shard_map/ppermute | solution.py:413
  36.9 21.5 %collective-permute-start.5 = (bf16[2,2,256,128]{3,2,1,0:T(8,128)(2,1)}, bf16[2,2,256,128]{3,2,1,0:T(8,128)(2,1)}, u32[]{:S(2)}, u32[]{:S(2)}) collective-permute-start(bf16[2,2,256,128]{3,2,1,0:T(8,128)(2,1)} %collective-permute-done.rest_1_), channel_id=1, source_target_pairs={{0,2},{1,3},{2,0},{3,1},{4,6},{5,7},{6,4},{7,5},{8,10},{9,11},{10,... | collective-permute-start | bytes 786440 | tf_op jit(solution)/shard_map/ppermute | solution.py:413
  38.3 20.2 %collective-permute-start.7 = (bf16[2,2,256,128]{3,2,1,0:T(8,128)(2,1)}, bf16[2,2,256,128]{3,2,1,0:T(8,128)(2,1)}, u32[]{:S(2)}, u32[]{:S(2)}) collective-permute-start(bf16[2,2,256,128]{3,2,1,0:T(8,128)(2,1)} %collective-permute-done.rest_1_), channel_id=1, source_target_pairs={{0,1},{1,0},{2,3},{3,2},{4,5},{5,4},{6,7},{7,6},{8,9},{9,8},{10,11... | collective-permute-start | bytes 786440 | tf_op jit(solution)/shard_map/ppermute | solution.py:413
  43.0 1.0 %copy-start.5 = (bf16[2,2,256,128]{3,2,1,0:T(8,128)(2,1)S(1)}, bf16[2,2,256,128]{3,2,1,0:T(8,128)(2,1)}, u32[]{:S(2)}) copy-start(bf16[2,2,256,128]{3,2,1,0:T(8,128)(2,1)} %copy-done.4) | copy-start | bytes 786436
  44.0 0.9 %copy-start.7 = (bf16[2,2,256,128]{3,2,1,0:T(8,128)(2,1)S(1)}, bf16[2,2,256,128]{3,2,1,0:T(8,128)(2,1)}, u32[]{:S(2)}) copy-start(bf16[2,2,256,128]{3,2,1,0:T(8,128)(2,1)} %copy-done.6) | copy-start | bytes 786436
  44.9 0.9 %copy-start.9 = (f32[2,256,128]{2,1,0:T(8,128)S(1)}, f32[2,256,128]{2,1,0:T(8,128)}, u32[]{:S(2)}) copy-start(f32[2,256,128]{2,1,0:T(8,128)} %copy-done.8) | copy-start | bytes 786436

commit v5 on v4

--- a/solution.py
+++ b/solution.py
@@ -428,7 +428,7 @@
 
     order = sorted(range(dec_size), key=lambda j: (j % group, j // group))
     attends = functools.partial(attend, rep_size=rep_size, per_group=per_group, qpos=qpos, positions=positions)
-    hops = [1] + list(range(rep_size - 1, 1, -1))
+    hops = [1] + list(range(2, rep_size))
     own = {r: swap(kv, "rep", rep_size, r) for r in hops}
     for j in order[:2]:
         hand_over(j, near[-1])

time: 71.1 us -> 71.6 us (level)
  the two profiles are of different devices: /device:TPU:1 before, /device:TPU:11 now
where the time goes in v5:
time: 71.6 us; the launch traced here: 70.7 us
  Pallas kernels  35 us (49%)
  waiting for transfers between devices  16.1 us (22%)
  starting transfers between devices  12.6 us (18%)
  local copies, waits for them, and re-layouts  6.21 us (9%)
  between operations  0.78 us (1%)
    pallas_call x3, Pallas kernels, attend(): pl.pallas_call(functools.partial(attend_kernel, moves, rep_size, first, l...  20 us
    ppermute x7, waiting for transfers between devices, shards(): lax.ppermute(value, axis, [(i, i ^ hop) for i in range(size)])  12 us
    ppermute x7, starting transfers between devices, shards(): lax.ppermute(value, axis, [(i, i ^ hop) for i in range(size)])  8.14 us
    pallas_call x2, Pallas kernels, place(): pl.pallas_call(functools.partial(place_kernel, dims, here, rest_j), out_s...  6.47 us
    unnamed x22, local copies, waits for them, and re-layouts  6.21 us
    ppermute x4, starting transfers between devices, hand_over(): arrived[j] = lax.ppermute(after(sends[j], *before), ('pre', 'dec'), route)  4.46 us
    ppermute x4, waiting for transfers between devices, hand_over(): arrived[j] = lax.ppermute(after(sends[j], *before), ('pre', 'dec'), route)  4.06 us
    pallas_call x1, Pallas kernels, pack(): pl.pallas_call(functools.partial(pack_kernel, dims), out_shape=[jax.Shape...  3.11 us
  transfers between devices with their start and end apart: 11, of which 4 were waited for; matrix products, arithmetic and copies ran while one was open for 0% of the time, Pallas kernels for 42%

profile of v5, /device:TPU:11, one launch (start us, length us, event | category | flops | bytes accessed | tf_op | source)
XLA Modules:
  0.0 70.7 jit_solution(18444339001968437503)
XLA Ops:
  0.6 2.6 %turn.1 = (bf16[2,2,256,128]{3,2,1,0:T(8,128)(2,1)}, f32[256,128]{1,0:T(8,128)}, f32[256,128]{1,0:T(8,128)}, s32[256,128]{1,0:T(8,128)}) custom-call(s32[16,128]{1,0:T(8,128)} %bitcast.4, f32[1,128]{1,0:T(1,128)} %constant.2.clone.freq_ref, f32[1,1024]{1,0:T(1,128)} %bitcast.9, f32[1,1024]{1,0:T(1,128)} %bitcast.10, bf16[256,1024]{1,0:T(8,128)(2,1)} %keys_hbm.1, ...), custom_call_target="tpu_custom_call" | custom-call | flops 1 | bytes 1 | tf_op jit(solution)/shard_map/turn/pallas_call | solution.py:86
  3.2 0.0 copy-start.10
  3.3 1.3 %collective-permute-start = (bf16[2,2,256,128]{3,2,1,0:T(8,128)(2,1)}, bf16[2,2,256,128]{3,2,1,0:T(8,128)(2,1)}, u32[]{:S(2)}, u32[]{:S(2)}) collective-permute-start(bf16[2,2,256,128]{3,2,1,0:T(8,128)(2,1)} %get-tuple-element.26.rest_0_.kv_hbm), channel_id=1, source_target_pairs={{0,16},{16,0},{1,17},{17,1},{2,18},{18,2},{3,19},{19,3},{4,20},{20... | collective-permute-start | bytes 786440 | tf_op jit(solution)/shard_map/ppermute | solution.py:413
  4.6 2.3 %collective-permute-start.8 = (bf16[2,2,256,128]{3,2,1,0:T(8,128)(2,1)}, bf16[2,2,256,128]{3,2,1,0:T(8,128)(2,1)S(1)}, u32[]{:S(2)}, u32[]{:S(2)}) collective-permute-start(bf16[2,2,256,128]{3,2,1,0:T(8,128)(2,1)} %get-tuple-element.26.rest_0_.kv_hbm), channel_id=1, source_target_pairs={{0,2},{1,3},{2,0},{3,1},{4,6},{5,7},{6,4},{7,5},{8,10},{9,11},{10,... | collective-permute-start | bytes 786440 | tf_op jit(solution)/shard_map/ppermute | solution.py:413
  6.9 1.2 %collective-permute-start.1 = (bf16[2,2,256,128]{3,2,1,0:T(8,128)(2,1)}, bf16[2,2,256,128]{3,2,1,0:T(8,128)(2,1)S(1)}, u32[]{:S(2)}, u32[]{:S(2)}) collective-permute-start(bf16[2,2,256,128]{3,2,1,0:T(8,128)(2,1)} %get-tuple-element.26.rest_0_.kv_hbm), channel_id=1, source_target_pairs={{0,1},{1,0},{2,3},{3,2},{4,5},{5,4},{6,7},{7,6},{8,9},{9,8},{10,11... | collective-permute-start | bytes 786440 | tf_op jit(solution)/shard_map/ppermute | solution.py:413
  8.1 3.1 %pack.1 = (bf16[4,4,4,64,128]{4,3,2,1,0:T(8,128)(2,1)}, bf16[4,4,4,64,128]{4,3,2,1,0:T(8,128)(2,1)}, bf16[4,4,4,64,128]{4,3,2,1,0:T(8,128)(2,1)}, bf16[4,4,4,64,128]{4,3,2,1,0:T(8,128)(2,1)}) custom-call(s32[4,16]{1,0:T(4,128)} %page_ref.5, s32[32]{0:T(128)} %lengths_ref.1, s32[32]{0:T(128)} %replica_ref.1, ...), custom_call_target="tpu_custom_call" | custom-call | flops 1 | bytes 1 | tf_op jit(solution)/shard_map/pack/pallas_call | solution.py:170
  11.2 0.0 collective-permute-done.rest_1_
  11.2 2.7 %collective-permute-start.4 = (bf16[4,4,4,64,128]{4,3,2,1,0:T(8,128)(2,1)}, bf16[4,4,4,64,128]{4,3,2,1,0:T(8,128)(2,1)}, u32[]{:S(2)}, u32[]{:S(2)}) collective-permute-start(bf16[4,4,4,64,128]{4,3,2,1,0:T(8,128)(2,1)} %get-tuple-element.30.own_hbm), channel_id=1, source_target_pairs={{8,16},{12,20},{16,8},{20,12},{9,17},{13,21},{17,9},{21,13},{10,18... | collective-permute-start | bytes 3145736 | tf_op jit(solution)/shard_map/ppermute | solution.py:427
  13.9 0.1 collective-permute-start.6
  14.0 2.9 %rotate_queries.1.query_ref = bf16[16,256,128]{2,1,0:T(8,128)(2,1)} custom-call(bf16[256,2048]{1,0:T(8,128)(2,1)} %query_ref.1, f32[1,2048]{1,0:T(1,128)} %bitcast.8, f32[256,128]{1,0:T(8,128)} %get-tuple-element.23.cos_ref, f32[256,128]{1,0:T(8,128)} %get-tuple-element.24.sin_ref), custom_call_target="tpu_custom_call" | custom-call | flops 1 | bytes 1 | tf_op jit(solution)/shard_map/rotate_queries/pallas_call | solution.py:200
  16.9 0.0 copy-start
  16.9 1.2 %copy-done = bf16[16,256,128]{2,1,0:T(8,128)(2,1)S(1)} copy-done((bf16[16,256,128]{2,1,0:T(8,128)(2,1)S(1)}, bf16[16,256,128]{2,1,0:T(8,128)(2,1)}, u32[]{:S(2)}) %copy-start) | copy-done | bytes 1048600
  18.1 4.4 %attend.3 = (f32[2,256,128]{2,1,0:T(8,128)S(1)}, f32[16,256,128]{2,1,0:T(8,128)S(1)}) custom-call(bf16[16,256,128]{2,1,0:T(8,128)(2,1)S(1)} %copy-done, s32[256,128]{1,0:T(8,128)S(1)} %copy-done.2, s32[16,128]{1,0:T(8,128)S(1)} %bitcast.5, bf16[2,2,256,128]{3,2,1,0:T(8,128)(2,1)S(1)} %copy-done.3, bf16[2,2,256,128]{3,2,1,0:T(8,128)(2,1)} %collective-permute-done.rest_1_), custom_call_target="tpu_custom_call" | custom-call | flops 1 | bytes 1 | tf_op jit(solution)/shard_map/attend/pallas_call | solution.py:285
  22.5 0.7 copy-done.8
  23.2 1.2 %collective-permute-done.8.rest_1_ = bf16[2,2,256,128]{3,2,1,0:T(8,128)(2,1)S(1)} collective-permute-done((bf16[2,2,256,128]{3,2,1,0:T(8,128)(2,1)}, bf16[2,2,256,128]{3,2,1,0:T(8,128)(2,1)S(1)}, u32[]{:S(2)}, u32[]{:S(2)}) %collective-permute-start.8) | collective-permute-done | bytes 262176 | tf_op jit(solution)/shard_map/ppermute | solution.py:413
  24.4 5.6 %collective-permute-done.3.rest_2_ = bf16[2,2,256,128]{3,2,1,0:T(8,128)(2,1)S(1)} collective-permute-done((bf16[2,2,256,128]{3,2,1,0:T(8,128)(2,1)}, bf16[2,2,256,128]{3,2,1,0:T(8,128)(2,1)S(1)}, u32[]{:S(2)}, u32[]{:S(2)}) %collective-permute-start.3) | collective-permute-done | bytes 262176 | tf_op jit(solution)/shard_map/ppermute | solution.py:413
  30.0 0.7 %copy-done.4 = bf16[2,2,256,128]{3,2,1,0:T(8,128)(2,1)} copy-done((bf16[2,2,256,128]{3,2,1,0:T(8,128)(2,1)}, bf16[2,2,256,128]{3,2,1,0:T(8,128)(2,1)S(1)}, u32[]{:S(2)}) %copy-start.4) | copy-done | bytes 262168
  30.7 0.7 copy-done.6
  31.4 0.6 collective-permute-start.10
  32.1 1.1 %collective-permute-start.9 = (bf16[4,4,4,64,128]{4,3,2,1,0:T(8,128)(2,1)}, bf16[4,4,4,64,128]{4,3,2,1,0:T(8,128)(2,1)}, u32[]{:S(2)}, u32[]{:S(2)}) collective-permute-start(bf16[4,4,4,64,128]{4,3,2,1,0:T(8,128)(2,1)} %get-tuple-element.40), channel_id=1, source_target_pairs={{0,4},{4,0},{8,20},{12,16},{16,12},{20,8},{24,28},{28,24},{1,5},{5... | collective-permute-start | bytes 3145736 | tf_op jit(solution)/shard_map/ppermute | solution.py:427
  33.2 4.0 %collective-permute-done.4.rest_0_ = bf16[4,4,4,64,128]{4,3,2,1,0:T(8,128)(2,1)} collective-permute-done((bf16[4,4,4,64,128]{4,3,2,1,0:T(8,128)(2,1)}, bf16[4,4,4,64,128]{4,3,2,1,0:T(8,128)(2,1)}, u32[]{:S(2)}, u32[]{:S(2)}) %collective-permute-start.4) | collective-permute-done | bytes 1048608 | tf_op jit(solution)/shard_map/ppermute | solution.py:427
  37.2 1.3 %collective-permute-start.5 = (bf16[2,2,256,128]{3,2,1,0:T(8,128)(2,1)}, bf16[2,2,256,128]{3,2,1,0:T(8,128)(2,1)}, u32[]{:S(2)}, u32[]{:S(2)}) collective-permute-start(bf16[2,2,256,128]{3,2,1,0:T(8,128)(2,1)} %collective-permute-done.rest_1_), channel_id=1, source_target_pairs={{0,3},{1,2},{2,1},{3,0},{4,7},{5,6},{6,5},{7,4},{8,11},{9,10},{10,... | collective-permute-start | bytes 786440 | tf_op jit(solution)/shard_map/ppermute | solution.py:413
  38.6 1.9 %collective-permute-start.7 = (bf16[2,2,256,128]{3,2,1,0:T(8,128)(2,1)}, bf16[2,2,256,128]{3,2,1,0:T(8,128)(2,1)}, u32[]{:S(2)}, u32[]{:S(2)}) collective-permute-start(bf16[2,2,256,128]{3,2,1,0:T(8,128)(2,1)} %collective-permute-done.rest_1_), channel_id=1, source_target_pairs={{0,1},{1,0},{2,3},{3,2},{4,5},{5,4},{6,7},{7,6},{8,9},{9,8},{10,11... | collective-permute-start | bytes 786440 | tf_op jit(solution)/shard_map/ppermute | solution.py:413
  40.5 3.7 %place.2.rest_2_ = bf16[1,1,8,8,4,64,128]{6,5,4,3,2,1,0:T(8,128)(2,1)} custom-call(s32[4,16]{1,0:T(4,128)} %page_ref.5, bf16[4,4,4,64,128]{4,3,2,1,0:T(8,128)(2,1)} %get-tuple-element.30.own_hbm, bf16[4,4,4,64,128]{4,3,2,1,0:T(8,128)(2,1)} %collective-permute-done.4.rest_0_, bf16[4,4,4,64,128]{4,3,2,1,0:T(8,128)(2,1)} %collective-permute-done.6.rest_1_), custom_call_target="tpu_custom_call" | custom-call | flops 1 | bytes 1 | tf_op jit(solution)/shard_map/place/pallas_call | solution.py:369
  44.2 0.9 %copy-done.5 = bf16[2,2,256,128]{3,2,1,0:T(8,128)(2,1)S(1)} copy-done((bf16[2,2,256,128]{3,2,1,0:T(8,128)(2,1)S(1)}, bf16[2,2,256,128]{3,2,1,0:T(8,128)(2,1)}, u32[]{:S(2)}) %copy-start.5) | copy-done | bytes 262168
  45.2 0.9 %copy-done.7 = bf16[2,2,256,128]{3,2,1,0:T(8,128)(2,1)S(1)} copy-done((bf16[2,2,256,128]{3,2,1,0:T(8,128)(2,1)S(1)}, bf16[2,2,256,128]{3,2,1,0:T(8,128)(2,1)}, u32[]{:S(2)}) %copy-start.7) | copy-done | bytes 262168
  46.1 0.9 %copy-done.9 = f32[2,256,128]{2,1,0:T(8,128)S(1)} copy-done((f32[2,256,128]{2,1,0:T(8,128)S(1)}, f32[2,256,128]{2,1,0:T(8,128)}, u32[]{:S(2)}) %copy-start.9) | copy-done | bytes 262168
  47.1 7.0 %attend.4 = (f32[2,256,128]{2,1,0:T(8,128)S(1)}, f32[16,256,128]{2,1,0:T(8,128)S(1)}) custom-call(bf16[16,256,128]{2,1,0:T(8,128)(2,1)S(1)} %copy-done.1, s32[256,128]{1,0:T(8,128)S(1)} %copy-done.2, s32[16,128]{1,0:T(8,128)S(1)} %bitcast.6, bf16[2,2,256,128]{3,2,1,0:T(8,128)(2,1)S(1)} %copy-done.7, ...), custom_call_target="tpu_custom_call" | custom-call | flops 1 | bytes 1 | tf_op jit(solution)/shard_map/attend/pallas_call | solution.py:285
  54.1 5.2 %collective-permute-done.5.rest_1_ = bf16[2,2,256,128]{3,2,1,0:T(8,128)(2,1)} collective-permute-done((bf16[2,2,256,128]{3,2,1,0:T(8,128)(2,1)}, bf16[2,2,256,128]{3,2,1,0:T(8,128)(2,1)}, u32[]{:S(2)}, u32[]{:S(2)}) %collective-permute-start.5) | collective-permute-done | bytes 262176 | tf_op jit(solution)/shard_map/ppermute | solution.py:413
  59.2 8.7 %attend.5 = bf16[256,2048]{1,0:T(8,128)(2,1)} custom-call(bf16[16,256,128]{2,1,0:T(8,128)(2,1)S(1)} %copy-done.1, s32[256,128]{1,0:T(8,128)S(1)} %copy-done.2, s32[16,128]{1,0:T(8,128)S(1)} %bitcast.7, bf16[2,2,256,128]{3,2,1,0:T(8,128)(2,1)} %collective-permute-done.2.rest_0_, bf16[2,2,256,128]{3,2,1,0:T(8,128)(2,1)} %collective-permute-done.5.rest_1_, ...), custom_call_target="tpu_custom_call" | custom-call | flops 1 | bytes 1 | tf_op jit(solution)/shard_map/attend/pallas_call | solution.py:285
  67.9 0.0 collective-permute-done.10.rest_1_
  67.9 2.8 %place.3 = bf16[1,1,8,8,4,64,128]{6,5,4,3,2,1,0:T(8,128)(2,1)} custom-call(s32[4,16]{1,0:T(4,128)} %page_ref.5, bf16[4,4,4,64,128]{4,3,2,1,0:T(8,128)(2,1)} %get-tuple-element.30.own_hbm, bf16[4,4,4,64,128]{4,3,2,1,0:T(8,128)(2,1)} %collective-permute-done.9.rest_0_, ...), custom_call_target="tpu_custom_call", output_to_operand_aliasing={{}: (4, {})} | custom-call | flops 1 | bytes 1 | tf_op jit(solution)/shard_map/place/pallas_call | solution.py:369
  (20 shorter events, 0.0 us)
Async XLA Ops:
  3.2 13.6 %copy-start.2 = (s32[256,128]{1,0:T(8,128)S(1)}, s32[256,128]{1,0:T(8,128)}, u32[]{:S(2)}) copy-start(s32[256,128]{1,0:T(8,128)} %get-tuple-element.25.qpos_ref) | copy-start | bytes 393220
  3.2 13.6 %copy-start.3 = (bf16[2,2,256,128]{3,2,1,0:T(8,128)(2,1)S(1)}, bf16[2,2,256,128]{3,2,1,0:T(8,128)(2,1)}, u32[]{:S(2)}) copy-start(bf16[2,2,256,128]{3,2,1,0:T(8,128)(2,1)} %get-tuple-element.26.rest_0_.kv_hbm) | copy-start | bytes 786436
  3.2 13.6 %copy-start.10 = (s32[2048]{0:T(1024)S(1)}, s32[2048]{0:T(1024)}, u32[]{:S(2)}) copy-start(s32[2048]{0:T(1024)} %param.18) | copy-start | bytes 24580
  3.3 8.0 %collective-permute-start = (bf16[2,2,256,128]{3,2,1,0:T(8,128)(2,1)}, bf16[2,2,256,128]{3,2,1,0:T(8,128)(2,1)}, u32[]{:S(2)}, u32[]{:S(2)}) collective-permute-start(bf16[2,2,256,128]{3,2,1,0:T(8,128)(2,1)} %get-tuple-element.26.rest_0_.kv_hbm), channel_id=1, source_target_pairs={{0,16},{16,0},{1,17},{17,1},{2,18},{18,2},{3,19},{19,3},{4,20},{20... | collective-permute-start | bytes 786440 | tf_op jit(solution)/shard_map/ppermute | solution.py:413
  4.6 19.8 %collective-permute-start.8 = (bf16[2,2,256,128]{3,2,1,0:T(8,128)(2,1)}, bf16[2,2,256,128]{3,2,1,0:T(8,128)(2,1)S(1)}, u32[]{:S(2)}, u32[]{:S(2)}) collective-permute-start(bf16[2,2,256,128]{3,2,1,0:T(8,128)(2,1)} %get-tuple-element.26.rest_0_.kv_hbm), channel_id=1, source_target_pairs={{0,2},{1,3},{2,0},{3,1},{4,6},{5,7},{6,4},{7,5},{8,10},{9,11},{10,... | collective-permute-start | bytes 786440 | tf_op jit(solution)/shard_map/ppermute | solution.py:413
  6.9 23.1 %collective-permute-start.3 = (bf16[2,2,256,128]{3,2,1,0:T(8,128)(2,1)}, bf16[2,2,256,128]{3,2,1,0:T(8,128)(2,1)S(1)}, u32[]{:S(2)}, u32[]{:S(2)}) collective-permute-start(bf16[2,2,256,128]{3,2,1,0:T(8,128)(2,1)} %get-tuple-element.26.rest_0_.kv_hbm), channel_id=1, source_target_pairs={{0,3},{1,2},{2,1},{3,0},{4,7},{5,6},{6,5},{7,4},{8,11},{9,10},{10,... | collective-permute-start | bytes 786440 | tf_op jit(solution)/shard_map/ppermute | solution.py:413
  6.9 23.9 %collective-permute-start.1 = (bf16[2,2,256,128]{3,2,1,0:T(8,128)(2,1)}, bf16[2,2,256,128]{3,2,1,0:T(8,128)(2,1)S(1)}, u32[]{:S(2)}, u32[]{:S(2)}) collective-permute-start(bf16[2,2,256,128]{3,2,1,0:T(8,128)(2,1)} %get-tuple-element.26.rest_0_.kv_hbm), channel_id=1, source_target_pairs={{0,1},{1,0},{2,3},{3,2},{4,5},{5,4},{6,7},{7,6},{8,9},{9,8},{10,11... | collective-permute-start | bytes 786440 | tf_op jit(solution)/shard_map/ppermute | solution.py:413
  11.2 26.0 %collective-permute-start.4 = (bf16[4,4,4,64,128]{4,3,2,1,0:T(8,128)(2,1)}, bf16[4,4,4,64,128]{4,3,2,1,0:T(8,128)(2,1)}, u32[]{:S(2)}, u32[]{:S(2)}) collective-permute-start(bf16[4,4,4,64,128]{4,3,2,1,0:T(8,128)(2,1)} %get-tuple-element.30.own_hbm), channel_id=1, source_target_pairs={{8,16},{12,20},{16,8},{20,12},{9,17},{13,21},{17,9},{21,13},{10,18... | collective-permute-start | bytes 3145736 | tf_op jit(solution)/shard_map/ppermute | solution.py:427
  13.9 24.6 %collective-permute-start.6 = (bf16[4,4,4,64,128]{4,3,2,1,0:T(8,128)(2,1)}, bf16[4,4,4,64,128]{4,3,2,1,0:T(8,128)(2,1)}, u32[]{:S(2)}, u32[]{:S(2)}) collective-permute-start(bf16[4,4,4,64,128]{4,3,2,1,0:T(8,128)(2,1)} %get-tuple-element.33), channel_id=1, source_target_pairs={{0,8},{4,12},{8,24},{12,28},{16,0},{20,4},{24,16},{28,20},{1,9},{5... | collective-permute-start | bytes 3145736 | tf_op jit(solution)/shard_map/ppermute | solution.py:427
  16.9 1.2 %copy-start = (bf16[16,256,128]{2,1,0:T(8,128)(2,1)S(1)}, bf16[16,256,128]{2,1,0:T(8,128)(2,1)}, u32[]{:S(2)}) copy-start(bf16[16,256,128]{2,1,0:T(8,128)(2,1)} %rotate_queries.1.query_ref) | copy-start | bytes 3145732
  22.5 0.7 copy-start.8
  30.0 0.7 %copy-start.4 = (bf16[2,2,256,128]{3,2,1,0:T(8,128)(2,1)}, bf16[2,2,256,128]{3,2,1,0:T(8,128)(2,1)S(1)}, u32[]{:S(2)}) copy-start(bf16[2,2,256,128]{3,2,1,0:T(8,128)(2,1)S(1)} %collective-permute-done.3.rest_2_) | copy-start | bytes 786436
  30.7 0.7 copy-start.6
  31.4 12.8 %copy-start.1 = (bf16[16,256,128]{2,1,0:T(8,128)(2,1)S(1)}, bf16[16,256,128]{2,1,0:T(8,128)(2,1)}, u32[]{:S(2)}) copy-start(bf16[16,256,128]{2,1,0:T(8,128)(2,1)} %rotate_queries.1.query_ref) | copy-start | bytes 3145732
  31.4 36.5 %collective-permute-start.10 = (bf16[4,4,4,64,128]{4,3,2,1,0:T(8,128)(2,1)}, bf16[4,4,4,64,128]{4,3,2,1,0:T(8,128)(2,1)}, u32[]{:S(2)}, u32[]{:S(2)}) collective-permute-start(bf16[4,4,4,64,128]{4,3,2,1,0:T(8,128)(2,1)} %get-tuple-element.42), channel_id=1, source_target_pairs={{0,12},{4,8},{8,28},{12,24},{16,4},{20,0},{24,20},{28,16},{1,13},{... | collective-permute-start | bytes 3145736 | tf_op jit(solution)/shard_map/ppermute | solution.py:427
  32.1 35.8 %collective-permute-start.9 = (bf16[4,4,4,64,128]{4,3,2,1,0:T(8,128)(2,1)}, bf16[4,4,4,64,128]{4,3,2,1,0:T(8,128)(2,1)}, u32[]{:S(2)}, u32[]{:S(2)}) collective-permute-start(bf16[4,4,4,64,128]{4,3,2,1,0:T(8,128)(2,1)} %get-tuple-element.40), channel_id=1, source_target_pairs={{0,4},{4,0},{8,20},{12,16},{16,12},{20,8},{24,28},{28,24},{1,5},{5... | collective-permute-start | bytes 3145736 | tf_op jit(solution)/shard_map/ppermute | solution.py:427
  33.2 20.9 %collective-permute-start.2 = (bf16[2,2,256,128]{3,2,1,0:T(8,128)(2,1)}, bf16[2,2,256,128]{3,2,1,0:T(8,128)(2,1)}, u32[]{:S(2)}, u32[]{:S(2)}) collective-permute-start(bf16[2,2,256,128]{3,2,1,0:T(8,128)(2,1)} %collective-permute-done.rest_1_), channel_id=1, source_target_pairs={{0,2},{1,3},{2,0},{3,1},{4,6},{5,7},{6,4},{7,5},{8,10},{9,11},{10,... | collective-permute-start | bytes 786440 | tf_op jit(solution)/shard_map/ppermute | solution.py:413
  37.2 22.0 %collective-permute-start.5 = (bf16[2,2,256,128]{3,2,1,0:T(8,128)(2,1)}, bf16[2,2,256,128]{3,2,1,0:T(8,128)(2,1)}, u32[]{:S(2)}, u32[]{:S(2)}) collective-permute-start(bf16[2,2,256,128]{3,2,1,0:T(8,128)(2,1)} %collective-permute-done.rest_1_), channel_id=1, source_target_pairs={{0,3},{1,2},{2,1},{3,0},{4,7},{5,6},{6,5},{7,4},{8,11},{9,10},{10,... | collective-permute-start | bytes 786440 | tf_op jit(solution)/shard_map/ppermute | solution.py:413
  38.6 20.7 %collective-permute-start.7 = (bf16[2,2,256,128]{3,2,1,0:T(8,128)(2,1)}, bf16[2,2,256,128]{3,2,1,0:T(8,128)(2,1)}, u32[]{:S(2)}, u32[]{:S(2)}) collective-permute-start(bf16[2,2,256,128]{3,2,1,0:T(8,128)(2,1)} %collective-permute-done.rest_1_), channel_id=1, source_target_pairs={{0,1},{1,0},{2,3},{3,2},{4,5},{5,4},{6,7},{7,6},{8,9},{9,8},{10,11... | collective-permute-start | bytes 786440 | tf_op jit(solution)/shard_map/ppermute | solution.py:413
  44.2 1.0 %copy-start.5 = (bf16[2,2,256,128]{3,2,1,0:T(8,128)(2,1)S(1)}, bf16[2,2,256,128]{3,2,1,0:T(8,128)(2,1)}, u32[]{:S(2)}) copy-start(bf16[2,2,256,128]{3,2,1,0:T(8,128)(2,1)} %copy-done.4) | copy-start | bytes 786436
  45.2 0.9 %copy-start.7 = (bf16[2,2,256,128]{3,2,1,0:T(8,128)(2,1)S(1)}, bf16[2,2,256,128]{3,2,1,0:T(8,128)(2,1)}, u32[]{:S(2)}) copy-start(bf16[2,2,256,128]{3,2,1,0:T(8,128)(2,1)} %copy-done.6) | copy-start | bytes 786436
  46.1 0.9 %copy-start.9 = (f32[2,256,128]{2,1,0:T(8,128)S(1)}, f32[2,256,128]{2,1,0:T(8,128)}, u32[]{:S(2)}) copy-start(f32[2,256,128]{2,1,0:T(8,128)} %copy-done.8) | copy-start | bytes 786436
